TPU v7x, 256 devices: a whole 4x4x8 slice. The times are simulated.
256 devices in a mesh: mode: 4 (over z_lo), ty: 8 (over y, core), tx: 8 (over z_hi, x).
Axes of the slice: x: 4, y: 4, z: 8 (z_hi: 2, z_lo: 4; z = z_hi * 4 + z_lo), core: 2. Of those that a mesh axis runs over, the one named last changes fastest.
Arguments:
- object_slices: float32 [4, 2, 1024, 1024], P(None, None, 'ty', 'tx'), may hold values from -4.2 to 4.2
- probe_modes: float32 [16, 2, 128, 128], P('mode'), may hold values from -1.5 to 1.5
- positions: int32 [8, 8, 1, 2], P('ty', 'tx'), may hold values from 0 to 128
- measured: float32 [8, 8, 1, 128, 128], P('ty', 'tx'), may hold values from 0.3 to 3
Outputs:
- object_gradient: float32 [4, 2, 1024, 1024], P('mode', None, 'ty', 'tx')
Inputs may be any that keep to these rules, and one draw needn't show every extreme that they name: `positions`: pattern k of tile (a, b) has its 128 x 128 window inside that tile's region, which reaches 64 pixels beyond the tile on every side.
All inputs are finite; a program needn't handle non-finite values.
Results may differ from a plain program's by a relative error of at most 0.00016.
Values sent between devices are 32-bit elements; how exact they have to be, the bound alone decides.
A program may use at most 64 MiB of HBM per device.

v0:
```python
import functools

import numpy as np
import jax
import jax.numpy as jnp
from jax import lax
from jax.experimental import pallas as pl
from jax.experimental.pallas import tpu as pltpu
from jax.sharding import PartitionSpec as P

DET = 128
SLICES = 4
MARGIN = 64
LOCAL = 4
RATE = 0.3
F32 = jnp.float32
BF16 = jnp.bfloat16


def real_block(matrix):
    return np.block([[matrix.real, matrix.imag], [-matrix.imag, matrix.real]])


def tables():
    counter = np.arange(DET)
    fourier = np.exp(-2j * np.pi * (np.outer(counter, counter) % DET) / DET) / np.sqrt(DET)
    frequency = np.where(counter < DET // 2, counter, counter - DET).astype(np.float64)
    chirp = np.exp(-1j * RATE * frequency**2 / DET)
    step = fourier.conj() @ (chirp[:, None] * fourier)
    step = (step + step.T) / 2
    out = []
    for matrix in (step, step.conj(), fourier, fourier.conj()):
        block = real_block(matrix).astype(np.float32)
        high = block.astype(jnp.bfloat16)
        low = (block - high.astype(np.float32)).astype(jnp.bfloat16)
        out += [high, low]
    return np.stack(out)


STEP, STEP_BACK, FAR, FAR_BACK = range(4)
CONJ = {STEP: STEP_BACK, STEP_BACK: STEP, FAR: FAR_BACK, FAR_BACK: FAR}


def halves(x):
    high = x.astype(BF16)
    return high, (x - high.astype(F32)).astype(BF16)


def rows(m):
    return slice(m * DET, (m + 1) * DET)


def right_product(mats, which, real, imag):
    rh, rl = halves(real)
    ih, il = halves(imag)
    lhs = jnp.concatenate([rh, ih, rl, il, rh, ih], axis=1)
    high, low = mats[2 * which], mats[2 * which + 1]
    rhs = jnp.concatenate([high, high, low], axis=0)
    return jnp.dot(lhs, rhs, preferred_element_type=F32)


def left_product(mats, which, stacked):
    conj = CONJ[which]
    high, low = mats[2 * conj], mats[2 * conj + 1]
    lhs = jnp.concatenate([high, high, low], axis=1)
    rhs = jnp.concatenate([stacked, stacked[: 2 * DET]], axis=0)
    return jnp.dot(lhs, rhs, preferred_element_type=F32)


def two_sided(mats, which, fetch, deliver, mid):
    for m in range(LOCAL):
        real, imag = fetch(m)
        out = right_product(mats, which, real, imag)
        rh, rl = halves(out[:, :DET])
        ih, il = halves(out[:, DET:])
        for part, value in enumerate((rh, ih, rl, il)):
            mid[rows(part), rows(m)] = value
    for pair in range(LOCAL // 2):
        out = left_product(mats, which, mid[:, pair * 2 * DET : (pair + 1) * 2 * DET])
        for k in range(2):
            deliver(2 * pair + k, out[:DET, rows(k)], out[DET:, rows(k)])


def forward_kernel(pos_ref, ext_ref, probe_ref, mats, window_ref, psi_ref, far_ref, part_ref, mid):
    row, col = pos_ref[0], pos_ref[1]
    shift = lax.rem(2 * DET - col, 2 * DET)
    group = jnp.minimum(row // 8, DET // 8 - 1)
    lift = DET + 8 - (row - 8 * group)
    for s in range(SLICES):
        for c in range(2):
            band = ext_ref[s, c, pl.ds(pl.multiple_of(8 * group, 8), DET + 8), :]
            band = pltpu.roll(band, lift, 0)[:DET]
            window_ref[s, c] = pltpu.roll(band, shift, 1)[:, :DET]
    for s in range(SLICES):

        def fetch(m):
            if s == 0:
                real, imag = probe_ref[m, 0], probe_ref[m, 1]
            else:
                real, imag = psi_ref[s - 1, 0, rows(m)], psi_ref[s - 1, 1, rows(m)]
            wr, wi = window_ref[s, 0], window_ref[s, 1]
            return real * wr - imag * wi, real * wi + imag * wr

        def deliver(m, real, imag):
            if s + 1 < SLICES:
                psi_ref[s, 0, rows(m)] = real
                psi_ref[s, 1, rows(m)] = imag
            else:
                far_ref[0, rows(m)] = real
                far_ref[1, rows(m)] = imag
                power = real * real + imag * imag
                part_ref[...] = power if m == 0 else part_ref[...] + power

        two_sided(mats, STEP if s + 1 < SLICES else FAR, fetch, deliver, mid)


def backward_kernel(window_ref, psi_ref, far_ref, probe_ref, whole_ref, measured_ref, mats, term_ref, pulled, mid):
    weight = 1.0 - measured_ref[...] / jnp.maximum(jnp.sqrt(whole_ref[...]), 1.0)
    for s in reversed(range(SLICES)):

        def fetch(m):
            if s == SLICES - 1:
                return weight * far_ref[0, rows(m)], weight * far_ref[1, rows(m)]
            return pulled[0, rows(m)], pulled[1, rows(m)]

        def deliver(m, real, imag):
            if s == 0:
                pr, pi = probe_ref[m, 0], probe_ref[m, 1]
            else:
                pr, pi = psi_ref[s - 1, 0, rows(m)], psi_ref[s - 1, 1, rows(m)]
            tr, ti = pr * real + pi * imag, pr * imag - pi * real
            term_ref[s, 0] = tr if m == 0 else term_ref[s, 0] + tr
            term_ref[s, 1] = ti if m == 0 else term_ref[s, 1] + ti
            if s > 0:
                wr, wi = window_ref[s, 0], window_ref[s, 1]
                pulled[0, rows(m)] = wr * real + wi * imag
                pulled[1, rows(m)] = wr * imag - wi * real

        two_sided(mats, FAR_BACK if s == SLICES - 1 else STEP_BACK, fetch, deliver, mid)


VMEM = pl.BlockSpec(memory_space=pltpu.VMEM)
SMEM = pl.BlockSpec(memory_space=pltpu.SMEM)


def forward(pos, ext, probe, mats):
    return pl.pallas_call(
        forward_kernel,
        out_shape=(
            jax.ShapeDtypeStruct((SLICES, 2, DET, DET), F32),
            jax.ShapeDtypeStruct((SLICES - 1, 2, LOCAL * DET, DET), F32),
            jax.ShapeDtypeStruct((2, LOCAL * DET, DET), F32),
            jax.ShapeDtypeStruct((DET, DET), F32),
        ),
        in_specs=[SMEM, VMEM, VMEM, VMEM],
        out_specs=(VMEM,) * 4,
        scratch_shapes=[pltpu.VMEM((4 * DET, LOCAL * DET), BF16)],
        name="forward",
    )(pos, ext, probe, mats)


def backward(window, psi, far, probe, whole, measured, mats):
    return pl.pallas_call(
        backward_kernel,
        out_shape=jax.ShapeDtypeStruct((SLICES, 2, DET, DET), F32),
        in_specs=[VMEM] * 7,
        out_specs=VMEM,
        scratch_shapes=[pltpu.VMEM((2, LOCAL * DET, DET), F32), pltpu.VMEM((4 * DET, LOCAL * DET), BF16)],
        name="backward",
    )(window, psi, far, probe, whole, measured, mats)


def shifted(block, axis, distance):
    devices = range(lax.axis_size(axis))
    route = [(i - distance, i) for i in devices if i - distance in devices]
    return lax.ppermute(block, axis, route)


def extended(shard, sides, width):
    for axis, dim in sides:
        size, length = (lax.axis_size(axis), shard.shape[dim])
        up = [(i, (i + 1) % size) for i in range(size - 1)]
        down = [(j, i) for i, j in up]
        last = lax.slice_in_dim(shard, length - width, length, axis=dim)
        leading = lax.slice_in_dim(shard, 0, width, axis=dim)
        before = lax.ppermute(last, axis, up)
        after = lax.ppermute(leading, axis, down)
        shard = jnp.concatenate([before, shard, after], axis=dim)
    return shard


def border_sum(gradient):
    upper = gradient[:, :, :MARGIN, :]
    lower = gradient[:, :, -MARGIN:, :]
    from_next = shifted(upper, "ty", -1)
    from_prior = shifted(lower, "ty", 1)
    middle = gradient[:, :, MARGIN:-MARGIN, :]
    middle = middle.at[:, :, :MARGIN, :].add(from_prior)
    middle = middle.at[:, :, -MARGIN:, :].add(from_next)
    left_strip = middle[:, :, :, :MARGIN]
    right_strip = middle[:, :, :, -MARGIN:]
    from_right = shifted(left_strip, "tx", -1)
    from_left = shifted(right_strip, "tx", 1)
    interior = middle[:, :, :, MARGIN:-MARGIN]
    interior = interior.at[:, :, :, :MARGIN].add(from_left)
    interior = interior.at[:, :, :, -MARGIN:].add(from_right)
    return interior


def body(object_slices, probe_modes, positions, measured):
    mats = jnp.asarray(tables())
    pos = positions.reshape(2)
    ext = extended(object_slices, (("ty", 2), ("tx", 3)), MARGIN)
    window, psi, far, part = forward(pos, ext, probe_modes, mats)
    copies = jnp.broadcast_to(part, (lax.axis_size("mode"), DET, DET))
    whole = jnp.sum(lax.all_to_all(copies, "mode", split_axis=0, concat_axis=0, tiled=True), axis=0)
    terms = backward(window, psi, far, probe_modes, whole, measured[0, 0, 0], mats)
    arrived = lax.all_to_all(terms, "mode", split_axis=0, concat_axis=0, tiled=True)
    mine = jnp.sum(arrived.reshape(lax.axis_size("mode"), 1, 2, DET, DET), axis=0)
    gradient = jnp.zeros((1, 2, 2 * DET, 2 * DET), F32)
    gradient = lax.dynamic_update_slice(gradient, mine, (0, 0, pos[0], pos[1]))
    return border_sum(gradient)


def solution(mesh):
    return jax.shard_map(
        body,
        mesh=mesh,
        in_specs=(
            P(None, None, "ty", "tx"),
            P("mode", None, None, None),
            P("ty", "tx", None, None),
            P("ty", "tx", None, None, None),
        ),
        out_specs=P("mode", None, "ty", "tx"),
        check_vma=False,
    )
```

profile of v0, /device:TPU:7, one launch (start us, length us, event | category | flops | bytes accessed | tf_op | source)
XLA Modules:
  0.0 129.0 jit_solution(17341815861268766382)
XLA Ops:
  0.0 1.1 fusion.4
  1.1 3.8 %collective-permute-start = (f32[4,2,64,128]{3,2,1,0:T(8,128)S(1)}, f32[4,2,64,128]{3,2,1,0:T(8,128)S(1)}, u32[]{:S(2)}, u32[]{:S(2)}) collective-permute-start(f32[4,2,64,128]{3,2,1,0:T(8,128)S(1)} %get-tuple-element.66), channel_id=1, source_target_pairs={{0,8},{8,16},{16,24},{24,32},{32,40},{40,48},{48,56},{1,9},{9,17},... | collective-permute-start | bytes 786440 | tf_op jit(solution)/shard_map/ppermute | solution.py:186
  4.8 1.9 %collective-permute-start.1 = (f32[4,2,64,128]{3,2,1,0:T(8,128)S(1)}, f32[4,2,64,128]{3,2,1,0:T(8,128)S(1)}, u32[]{:S(2)}, u32[]{:S(2)}) collective-permute-start(f32[4,2,64,128]{3,2,1,0:T(8,128)S(1)} %get-tuple-element.65), channel_id=1, source_target_pairs={{8,0},{16,8},{24,16},{32,24},{40,32},{48,40},{56,48},{9,1},{17,9},... | collective-permute-start | bytes 786440 | tf_op jit(solution)/shard_map/ppermute | solution.py:187
  6.8 1.4 %collective-permute-done = f32[4,2,64,128]{3,2,1,0:T(8,128)S(1)} collective-permute-done((f32[4,2,64,128]{3,2,1,0:T(8,128)S(1)}, f32[4,2,64,128]{3,2,1,0:T(8,128)S(1)}, u32[]{:S(2)}, u32[]{:S(2)}) %collective-permute-start) | collective-permute-done | bytes 262176 | tf_op jit(solution)/shard_map/ppermute | solution.py:186
  8.2 1.1 constant_dynamic-update-slice_fusion.1
  9.2 3.3 %collective-permute-done.1 = f32[4,2,64,128]{3,2,1,0:T(8,128)S(1)} collective-permute-done((f32[4,2,64,128]{3,2,1,0:T(8,128)S(1)}, f32[4,2,64,128]{3,2,1,0:T(8,128)S(1)}, u32[]{:S(2)}, u32[]{:S(2)}) %collective-permute-start.1) | collective-permute-done | bytes 262176 | tf_op jit(solution)/shard_map/ppermute | solution.py:187
  12.6 0.3 fusion.2
  12.9 1.1 copy.10
  14.0 8.7 %collective-permute-start.2 = (f32[4,2,256,64]{2,3,1,0:T(8,128)}, f32[4,2,256,64]{2,3,1,0:T(8,128)S(1)}, u32[]{:S(2)}, u32[]{:S(2)}) collective-permute-start(f32[4,2,256,64]{2,3,1,0:T(8,128)} %copy.10), channel_id=1, source_target_pairs={{0,1},{1,2},{2,3},{3,4},{4,5},{5,6},{6,7},{8,9},{9,10},{10,11},{11... | collective-permute-start | bytes 1572872 | tf_op jit(solution)/shard_map/ppermute | solution.py:186
  22.8 0.3 copy.11
  23.1 1.9 %collective-permute-start.3 = (f32[4,2,256,64]{2,3,1,0:T(8,128)S(1)}, f32[4,2,256,64]{2,3,1,0:T(8,128)}, u32[]{:S(2)}, u32[]{:S(2)}) collective-permute-start(f32[4,2,256,64]{2,3,1,0:T(8,128)S(1)} %copy.11), channel_id=1, source_target_pairs={{1,0},{2,1},{3,2},{4,3},{5,4},{6,5},{7,6},{9,8},{10,9},{11,10},{12... | collective-permute-start | bytes 1572872 | tf_op jit(solution)/shard_map/ppermute | solution.py:187
  25.0 6.0 %collective-permute-done.2 = f32[4,2,256,64]{2,3,1,0:T(8,128)S(1)} collective-permute-done((f32[4,2,256,64]{2,3,1,0:T(8,128)}, f32[4,2,256,64]{2,3,1,0:T(8,128)S(1)}, u32[]{:S(2)}, u32[]{:S(2)}) %collective-permute-start.2) | collective-permute-done | bytes 524320 | tf_op jit(solution)/shard_map/ppermute | solution.py:186
  31.0 0.3 copy.12
  31.3 10.0 %collective-permute-done.3 = f32[4,2,256,64]{2,3,1,0:T(8,128)} collective-permute-done((f32[4,2,256,64]{2,3,1,0:T(8,128)S(1)}, f32[4,2,256,64]{2,3,1,0:T(8,128)}, u32[]{:S(2)}, u32[]{:S(2)}) %collective-permute-start.3) | collective-permute-done | bytes 524320 | tf_op jit(solution)/shard_map/ppermute | solution.py:187
  41.3 1.4 %copy.13 = f32[4,2,256,64]{3,2,1,0:T(8,128)S(1)} copy(f32[4,2,256,64]{2,3,1,0:T(8,128)} %collective-permute-done.3) | data formatting | bytes 1048576 | tf_op jit(solution)/shard_map/ppermute | solution.py:187
  42.7 2.2 %pad_maximum_fusion.ext_ref = f32[4,2,256,256]{3,2,1,0:T(8,128)} fusion(f32[4,2,256,64]{3,2,1,0:T(8,128)S(1)} %copy.13, f32[4,2,256,128]{3,2,1,0:T(8,128)S(1)} %constant_dynamic-update-slice_fusion, f32[4,2,256,64]{3,2,1,0:T(8,128)S(1)} %copy.12), kind=kLoop, calls=%fused_computation | loop fusion | flops 1048576 | bytes 4194304 | tf_op jit(solution)/shard_map/concatenate | solution.py:188
  44.9 5.6 %forward.1 = (f32[4,2,128,128]{3,2,1,0:T(8,128)}, f32[3,2,512,128]{3,2,1,0:T(8,128)}, f32[2,512,128]{2,1,0:T(8,128)}, f32[128,128]{1,0:T(8,128)}) custom-call(s32[2]{0:T(128)} %bitcast.7, f32[4,2,256,256]{3,2,1,0:T(8,128)} %pad_maximum_fusion.ext_ref, f32[4,2,128,128]{3,2,1,0:T(8,128)} %probe_ref.3, bf16[8,256,256]{2,1,0:T(8,128)(2,1)} %constant.114.clone.mats), custom_call_target="tpu_custom_call" | custom-call | tf_op jit(solution)/shard_map/forward/pallas_call | solution.py:147
  50.5 0.9 broadcast_in_dim.7
  51.4 22.3 %all_to_all.10 = f32[4,128,128]{2,1,0:T(8,128)S(1)} all-to-all(f32[4,128,128]{2,1,0:T(8,128)S(1)} %broadcast_in_dim.7), channel_id=1, replica_groups=mesh['mode'=4,'ty'=8,'tx'=8] {'mode'}, dimensions={0} | all-to-all | bytes 524288 | tf_op jit(solution)/shard_map/all_to_all | solution.py:216
  73.7 0.6 reduce_sum.20.whole_ref
  74.3 0.0 copy-start.1
  74.3 5.8 %backward.1 = f32[4,2,128,128]{3,2,1,0:T(8,128)} custom-call(f32[4,2,128,128]{3,2,1,0:T(8,128)} %get-tuple-element.57.window_ref, f32[3,2,512,128]{3,2,1,0:T(8,128)} %get-tuple-element.58.psi_ref, f32[2,512,128]{2,1,0:T(8,128)} %get-tuple-element.59.far_ref, f32[4,2,128,128]{3,2,1,0:T(8,128)} %probe_ref.3, f32[128,128]{1,0:T(8,128)} %reduce_sum.20.whole_ref, ...), custom_call_target="tpu_custom_call" | custom-call | tf_op jit(solution)/shard_map/backward/pallas_call | solution.py:163
  80.1 3.5 %all-to-all-start.1 = ((f32[4,2,128,128]{3,2,1,0:T(8,128)}), f32[4,2,128,128]{3,2,1,0:T(8,128)S(1)}, u32[]{:S(2)}, u32[]{:S(2)}) async-start(f32[4,2,128,128]{3,2,1,0:T(8,128)} %backward.1), calls=%async_computation.1 | async-start | bytes 1048576 | tf_op jit(solution)/shard_map/all_to_all | solution.py:218
  83.6 0.0 copy-done.1
  83.6 0.6 fusion.6
  88.0 9.6 %all-to-all-done.1 = f32[4,2,128,128]{3,2,1,0:T(8,128)S(1)} async-done(((f32[4,2,128,128]{3,2,1,0:T(8,128)}), f32[4,2,128,128]{3,2,1,0:T(8,128)S(1)}, u32[]{:S(2)}, u32[]{:S(2)}) %all-to-all-start.1) | async-done | bytes 524320 | tf_op jit(solution)/shard_map/all_to_all | solution.py:218
  97.7 2.4 %dynamic_update_slice.3 = f32[1,2,256,256]{3,2,1,0:T(8,128)S(1)} dynamic-update-slice(f32[1,2,256,256]{3,2,1,0:T(8,128)S(1)} %broadcast_in_dim.6, f32[1,2,128,128]{3,2,1,0:T(8,128)S(1)} %bitcast.5, s32[]{:T(128)} %constant.111.clone.1, s32[]{:T(128)} %constant.111.clone.1, s32[]{:T(128)S(6)} %select_n.6, s32[]{:T(128)S(6)} %select_n.7) | dynamic-update-slice | bytes 262148 | tf_op jit(solution)/shard_map/dynamic_update_slice | solution.py:221
  100.1 6.7 %collective-permute-start.4 = (f32[1,2,64,256]{3,2,1,0:T(8,128)S(1)}, f32[1,2,64,256]{3,2,1,0:T(8,128)S(1)}, u32[]{:S(2)}, u32[]{:S(2)}) collective-permute-start(f32[1,2,64,256]{3,2,1,0:T(8,128)S(1)} %get-tuple-element.64), channel_id=1, source_target_pairs={{0,8},{8,16},{16,24},{24,32},{32,40},{40,48},{48,56},{1,9},{9,17},... | collective-permute-start | bytes 393224 | tf_op jit(solution)/shard_map/ppermute | solution.py:176
  106.8 1.9 %collective-permute-start.5 = (f32[1,2,64,256]{3,2,1,0:T(8,128)S(1)}, f32[1,2,64,256]{3,2,1,0:T(8,128)S(1)}, u32[]{:S(2)}, u32[]{:S(2)}) collective-permute-start(f32[1,2,64,256]{3,2,1,0:T(8,128)S(1)} %get-tuple-element.63), channel_id=1, source_target_pairs={{8,0},{16,8},{24,16},{32,24},{40,32},{48,40},{56,48},{9,1},{17,9},... | collective-permute-start | bytes 393224 | tf_op jit(solution)/shard_map/ppermute | solution.py:176
  108.8 0.0 collective-permute-done.4
  108.8 4.3 %collective-permute-done.5 = f32[1,2,64,256]{3,2,1,0:T(8,128)S(1)} collective-permute-done((f32[1,2,64,256]{3,2,1,0:T(8,128)S(1)}, f32[1,2,64,256]{3,2,1,0:T(8,128)S(1)}, u32[]{:S(2)}, u32[]{:S(2)}) %collective-permute-start.5) | collective-permute-done | bytes 131104 | tf_op jit(solution)/shard_map/ppermute | solution.py:176
  113.1 0.1 fusion.5
  113.2 1.9 %collective-permute-start.6 = (f32[1,2,128,64]{3,2,1,0:T(8,128)S(1)}, f32[1,2,128,64]{3,2,1,0:T(8,128)S(1)}, u32[]{:S(2)}, u32[]{:S(2)}) collective-permute-start(f32[1,2,128,64]{3,2,1,0:T(8,128)S(1)} %get-tuple-element.68), channel_id=1, source_target_pairs={{0,1},{1,2},{2,3},{3,4},{4,5},{5,6},{6,7},{8,9},{9,10},{10,11},{11... | collective-permute-start | bytes 196616 | tf_op jit(solution)/shard_map/ppermute | solution.py:176
  115.2 0.1 slice.179
  115.3 3.4 %collective-permute-start.7 = (f32[1,2,128,64]{3,2,1,0:T(8,128)S(1)}, f32[1,2,128,64]{3,2,1,0:T(8,128)S(1)}, u32[]{:S(2)}, u32[]{:S(2)}) collective-permute-start(f32[1,2,128,64]{3,2,1,0:T(8,128)S(1)} %get-tuple-element.67), channel_id=1, source_target_pairs={{1,0},{2,1},{3,2},{4,3},{5,4},{6,5},{7,6},{9,8},{10,9},{11,10},{12... | collective-permute-start | bytes 196616 | tf_op jit(solution)/shard_map/ppermute | solution.py:176
  118.6 0.3 collective-permute-done.6
  119.0 0.1 slice_add_fusion.1
  119.1 0.4 scatter-add.16
  119.5 0.0 copy-start
  119.5 7.6 %collective-permute-done.7 = f32[1,2,128,64]{3,2,1,0:T(8,128)S(1)} collective-permute-done((f32[1,2,128,64]{3,2,1,0:T(8,128)S(1)}, f32[1,2,128,64]{3,2,1,0:T(8,128)S(1)}, u32[]{:S(2)}, u32[]{:S(2)}) %collective-permute-start.7) | collective-permute-done | bytes 65568 | tf_op jit(solution)/shard_map/ppermute | solution.py:176
  127.1 0.1 slice_add_fusion
  127.2 0.0 copy-done
  127.2 1.8 %scatter-add.19 = f32[1,2,128,128]{3,2,1,0:T(8,128)} dynamic-update-slice(f32[1,2,128,128]{3,2,1,0:T(8,128)} %copy-done, f32[1,2,128,64]{3,2,1,0:T(8,128)S(1)} %slice_add_fusion, s32[]{:T(128)} %constant.111.clone.1, s32[]{:T(128)} %constant.111.clone.1, s32[]{:T(128)} %constant.111.clone.1, s32[]{:T(128)} %constant.113.clone.1) | dynamic-update-slice | bytes 131076 | tf_op jit(solution)/shard_map/scatter-add | solution.py:206
  (8 shorter events, 0.2 us)
Async XLA Ops:
  1.1 7.1 %collective-permute-start = (f32[4,2,64,128]{3,2,1,0:T(8,128)S(1)}, f32[4,2,64,128]{3,2,1,0:T(8,128)S(1)}, u32[]{:S(2)}, u32[]{:S(2)}) collective-permute-start(f32[4,2,64,128]{3,2,1,0:T(8,128)S(1)} %get-tuple-element.66), channel_id=1, source_target_pairs={{0,8},{8,16},{16,24},{24,32},{32,40},{40,48},{48,56},{1,9},{9,17},... | collective-permute-start | bytes 786440 | tf_op jit(solution)/shard_map/ppermute | solution.py:186
  4.8 7.7 %collective-permute-start.1 = (f32[4,2,64,128]{3,2,1,0:T(8,128)S(1)}, f32[4,2,64,128]{3,2,1,0:T(8,128)S(1)}, u32[]{:S(2)}, u32[]{:S(2)}) collective-permute-start(f32[4,2,64,128]{3,2,1,0:T(8,128)S(1)} %get-tuple-element.65), channel_id=1, source_target_pairs={{8,0},{16,8},{24,16},{32,24},{40,32},{48,40},{56,48},{9,1},{17,9},... | collective-permute-start | bytes 786440 | tf_op jit(solution)/shard_map/ppermute | solution.py:187
  14.0 17.0 %collective-permute-start.2 = (f32[4,2,256,64]{2,3,1,0:T(8,128)}, f32[4,2,256,64]{2,3,1,0:T(8,128)S(1)}, u32[]{:S(2)}, u32[]{:S(2)}) collective-permute-start(f32[4,2,256,64]{2,3,1,0:T(8,128)} %copy.10), channel_id=1, source_target_pairs={{0,1},{1,2},{2,3},{3,4},{4,5},{5,6},{6,7},{8,9},{9,10},{10,11},{11... | collective-permute-start | bytes 1572872 | tf_op jit(solution)/shard_map/ppermute | solution.py:186
  23.1 18.3 %collective-permute-start.3 = (f32[4,2,256,64]{2,3,1,0:T(8,128)S(1)}, f32[4,2,256,64]{2,3,1,0:T(8,128)}, u32[]{:S(2)}, u32[]{:S(2)}) collective-permute-start(f32[4,2,256,64]{2,3,1,0:T(8,128)S(1)} %copy.11), channel_id=1, source_target_pairs={{1,0},{2,1},{3,2},{4,3},{5,4},{6,5},{7,6},{9,8},{10,9},{11,10},{12... | collective-permute-start | bytes 1572872 | tf_op jit(solution)/shard_map/ppermute | solution.py:187
  74.3 9.3 %copy-start.1 = (s32[1,1,1,2]{3,2,1,0:T(1,128)S(1)}, s32[1,1,1,2]{3,2,1,0:T(1,128)}, u32[]{:S(2)}) copy-start(s32[1,1,1,2]{3,2,1,0:T(1,128)} %param.15) | copy-start | bytes 28
  80.1 17.5 %all-to-all-start.1 = ((f32[4,2,128,128]{3,2,1,0:T(8,128)}), f32[4,2,128,128]{3,2,1,0:T(8,128)S(1)}, u32[]{:S(2)}, u32[]{:S(2)}) async-start(f32[4,2,128,128]{3,2,1,0:T(8,128)} %backward.1), calls=%async_computation.1 | async-start | bytes 1048576 | tf_op jit(solution)/shard_map/all_to_all | solution.py:218
  100.1 8.6 %collective-permute-start.4 = (f32[1,2,64,256]{3,2,1,0:T(8,128)S(1)}, f32[1,2,64,256]{3,2,1,0:T(8,128)S(1)}, u32[]{:S(2)}, u32[]{:S(2)}) collective-permute-start(f32[1,2,64,256]{3,2,1,0:T(8,128)S(1)} %get-tuple-element.64), channel_id=1, source_target_pairs={{0,8},{8,16},{16,24},{24,32},{32,40},{40,48},{48,56},{1,9},{9,17},... | collective-permute-start | bytes 393224 | tf_op jit(solution)/shard_map/ppermute | solution.py:176
  106.8 6.3 %collective-permute-start.5 = (f32[1,2,64,256]{3,2,1,0:T(8,128)S(1)}, f32[1,2,64,256]{3,2,1,0:T(8,128)S(1)}, u32[]{:S(2)}, u32[]{:S(2)}) collective-permute-start(f32[1,2,64,256]{3,2,1,0:T(8,128)S(1)} %get-tuple-element.63), channel_id=1, source_target_pairs={{8,0},{16,8},{24,16},{32,24},{40,32},{48,40},{56,48},{9,1},{17,9},... | collective-permute-start | bytes 393224 | tf_op jit(solution)/shard_map/ppermute | solution.py:176
  113.2 5.7 %collective-permute-start.6 = (f32[1,2,128,64]{3,2,1,0:T(8,128)S(1)}, f32[1,2,128,64]{3,2,1,0:T(8,128)S(1)}, u32[]{:S(2)}, u32[]{:S(2)}) collective-permute-start(f32[1,2,128,64]{3,2,1,0:T(8,128)S(1)} %get-tuple-element.68), channel_id=1, source_target_pairs={{0,1},{1,2},{2,3},{3,4},{4,5},{5,6},{6,7},{8,9},{9,10},{10,11},{11... | collective-permute-start | bytes 196616 | tf_op jit(solution)/shard_map/ppermute | solution.py:176
  115.3 11.8 %collective-permute-start.7 = (f32[1,2,128,64]{3,2,1,0:T(8,128)S(1)}, f32[1,2,128,64]{3,2,1,0:T(8,128)S(1)}, u32[]{:S(2)}, u32[]{:S(2)}) collective-permute-start(f32[1,2,128,64]{3,2,1,0:T(8,128)S(1)} %get-tuple-element.67), channel_id=1, source_target_pairs={{1,0},{2,1},{3,2},{4,3},{5,4},{6,5},{7,6},{9,8},{10,9},{11,10},{12... | collective-permute-start | bytes 196616 | tf_op jit(solution)/shard_map/ppermute | solution.py:176
  119.5 7.7 %copy-start = (f32[1,2,128,128]{3,2,1,0:T(8,128)}, f32[1,2,128,128]{3,2,1,0:T(8,128)S(1)}, u32[]{:S(2)}) copy-start(f32[1,2,128,128]{3,2,1,0:T(8,128)S(1)} %scatter-add.16) | copy-start | bytes 393220
where the time goes:
time: 130 us; the launch traced here: 129 us
  waiting for transfers between devices  42.5 us (33%)
  starting transfers between devices  33.7 us (26%)
  blocking collectives  22.3 us (17%)
  local copies, waits for them, and re-layouts  12 us (9%)
  Pallas kernels  11.4 us (9%)
  between operations  4.03 us (3%)
  other arithmetic  3.14 us (2%)
    all_to_all x1, blocking collectives, body(): lax.all_to_all(copies, 'mode', split_axis=0, concat_axis=0, tiled=True)  22.3 us
    ppermute x4, starting transfers between devices, shifted(): return lax.ppermute(block, axis, route)  13.9 us
    ppermute x2, waiting for transfers between devices, extended(): after = lax.ppermute(leading, axis, down)  13.3 us
    ppermute x2, starting transfers between devices, extended(): before = lax.ppermute(last, axis, up)  12.5 us
    ppermute x4, waiting for transfers between devices, shifted(): return lax.ppermute(block, axis, route)  12.2 us
    all_to_all x1, waiting for transfers between devices, body(): lax.all_to_all(terms, 'mode', split_axis=0, concat_axis=0, tiled=True)  9.62 us
    ppermute x2, waiting for transfers between devices, extended(): before = lax.ppermute(last, axis, up)  7.36 us
    pallas_call x1, Pallas kernels, backward(): pl.pallas_call(backward_kernel, out_shape=jax.ShapeDtypeStruct((SLICES, 2...  5.8 us
  transfers between devices with their start and end apart: 9, of which 8 were waited for; matrix products, arithmetic and copies ran while one was open for 2% of the time, Pallas kernels for 0%

commit v1 on v0

v1 whole, which is shorter than its diff:
```python
import functools

import numpy as np
import jax
import jax.numpy as jnp
from jax import lax
from jax.experimental import pallas as pl
from jax.experimental.pallas import tpu as pltpu
from jax.sharding import PartitionSpec as P

DET = 128
SLICES = 4
MARGIN = 64
LOCAL = 4
RATE = 0.3
F32 = jnp.float32
BF16 = jnp.bfloat16


def real_block(matrix):
    return np.block([[matrix.real, matrix.imag], [-matrix.imag, matrix.real]])


def tables():
    counter = np.arange(DET)
    fourier = np.exp(-2j * np.pi * (np.outer(counter, counter) % DET) / DET) / np.sqrt(DET)
    frequency = np.where(counter < DET // 2, counter, counter - DET).astype(np.float64)
    chirp = np.exp(-1j * RATE * frequency**2 / DET)
    step = fourier.conj() @ (chirp[:, None] * fourier)
    step = (step + step.T) / 2
    out = []
    for matrix in (step, step.conj(), fourier, fourier.conj()):
        block = real_block(matrix).astype(np.float32)
        high = block.astype(jnp.bfloat16)
        low = (block - high.astype(np.float32)).astype(jnp.bfloat16)
        out += [high, low]
    return np.stack(out)


STEP, STEP_BACK, FAR, FAR_BACK = range(4)
CONJ = {STEP: STEP_BACK, STEP_BACK: STEP, FAR: FAR_BACK, FAR_BACK: FAR}


def halves(x):
    high = x.astype(BF16)
    return high, (x - high.astype(F32)).astype(BF16)


def rows(m):
    return slice(m * DET, (m + 1) * DET)


def right_product(mats, which, real, imag):
    rh, rl = halves(real)
    ih, il = halves(imag)
    lhs = jnp.concatenate([rh, ih, rl, il, rh, ih], axis=1)
    high, low = mats[2 * which], mats[2 * which + 1]
    rhs = jnp.concatenate([high, high, low], axis=0)
    return jnp.dot(lhs, rhs, preferred_element_type=F32)


def left_product(mats, which, stacked):
    conj = CONJ[which]
    high, low = mats[2 * conj], mats[2 * conj + 1]
    lhs = jnp.concatenate([high, high, low], axis=1)
    rhs = jnp.concatenate([stacked, stacked[: 2 * DET]], axis=0)
    return jnp.dot(lhs, rhs, preferred_element_type=F32)


def two_sided(mats, which, fetch, deliver, mid):
    for m in range(LOCAL):
        real, imag = fetch(m)
        out = right_product(mats, which, real, imag)
        rh, rl = halves(out[:, :DET])
        ih, il = halves(out[:, DET:])
        for part, value in enumerate((rh, ih, rl, il)):
            mid[rows(part), rows(m)] = value
    for pair in range(LOCAL // 2):
        out = left_product(mats, which, mid[:, pair * 2 * DET : (pair + 1) * 2 * DET])
        for k in range(2):
            deliver(2 * pair + k, out[:DET, rows(k)], out[DET:, rows(k)])


MESH = pl.DeviceIdType.MESH
HALF = DET // 2
BLOCK = HALF // 2


def lane_low(shape):
    return lax.broadcasted_iota(jnp.int32, shape, len(shape) - 1) < HALF


def turned(x):
    return pltpu.roll(x, HALF, x.ndim - 1)


def packed_edges(strip):
    first, second = strip[:BLOCK], strip[BLOCK:]
    low = lane_low(first.shape)
    left_edge = jnp.where(low, first, turned(second))
    right_edge = jnp.where(low, turned(first), second)
    return left_edge, right_edge


def unpacked_sides(from_left, from_right):
    low = lane_low(from_left.shape)
    first = jnp.where(low, from_right, turned(from_left))
    second = jnp.where(low, turned(from_right), from_left)
    return first, second


LEFT, RIGHT, UP, DOWN, UP_CORNER, DOWN_CORNER = range(6)


def kernel(
    pos_ref, obj, probe, measured, mats, out,
    pk, rs, vt, cr, ext, window, psi, far, part, others, mid, pulled, term, parts, grid, gv, middle, hp, gh,
    halo_send, halo_recv, mode_send, mode_recv, term_send, term_recv, grad_send, grad_recv,
):
    mode, ty, tx = lax.axis_index("mode"), lax.axis_index("ty"), lax.axis_index("tx")
    modes, tys, txs = lax.axis_size("mode"), lax.axis_size("ty"), lax.axis_size("tx")
    has = {LEFT: tx > 0, RIGHT: tx < txs - 1, UP: ty > 0, DOWN: ty < tys - 1}
    has[UP_CORNER], has[DOWN_CORNER] = has[UP], has[DOWN]
    cross_right, cross_left = tx == txs // 2 - 1, tx == txs // 2
    mirror = modes - 1 - mode
    left_mode = jnp.where(cross_left, mirror, mode)
    right_mode = jnp.where(cross_right, mirror, mode)
    target = {
        LEFT: {"mode": left_mode, "ty": ty, "tx": tx - 1},
        RIGHT: {"mode": right_mode, "ty": ty, "tx": tx + 1},
        UP: {"mode": mode, "ty": ty - 1, "tx": tx},
        DOWN: {"mode": mode, "ty": ty + 1, "tx": tx},
    }
    direct = {LEFT: {"mode": mode, "ty": ty, "tx": tx - 1}, RIGHT: {"mode": mode, "ty": ty, "tx": tx + 1}}

    def peer(step):
        return {"mode": lax.rem(mode + step, modes), "ty": ty, "tx": tx}

    for side in (LEFT, RIGHT):

        @pl.when(jnp.logical_not(has[side]))
        def _():
            rs[:, side] = jnp.zeros_like(rs[:, side])
            gh[side] = jnp.zeros_like(gh[side])

    for side in (UP, DOWN):

        @pl.when(jnp.logical_not(has[side]))
        def _():
            vt[:, side - UP] = jnp.zeros_like(vt[:, side - UP])
            cr[:, side - UP] = jnp.zeros_like(cr[:, side - UP])
            gv[side - UP] = jnp.zeros_like(gv[side - UP])

    for s in range(SLICES):
        for c in range(2):
            for b in range(2):
                left_edge, right_edge = packed_edges(obj[s, c, b * HALF : (b + 1) * HALF])
                pk[s, LEFT, c, b * BLOCK : (b + 1) * BLOCK] = left_edge
                pk[s, RIGHT, c, b * BLOCK : (b + 1) * BLOCK] = right_edge

    barrier = pltpu.get_barrier_semaphore()
    count = jnp.int32(modes - 1)
    for side in (LEFT, RIGHT, UP, DOWN):
        count = count + has[side].astype(jnp.int32)

        @pl.when(has[side])
        def _():
            pl.semaphore_signal(barrier, inc=1, device_id=target[side], device_id_type=MESH)

    for side, cross in ((LEFT, cross_left), (RIGHT, cross_right)):
        far_pair = jnp.logical_and(cross, has[side])
        count = count + far_pair.astype(jnp.int32)

        @pl.when(far_pair)
        def _():
            pl.semaphore_signal(barrier, inc=1, device_id=direct[side], device_id_type=MESH)

    for step in range(1, modes):
        pl.semaphore_signal(barrier, inc=1, device_id=peer(step), device_id_type=MESH)
    pl.semaphore_wait(barrier, count)

    opposite = {LEFT: RIGHT, RIGHT: LEFT, UP: DOWN, DOWN: UP, UP_CORNER: DOWN_CORNER, DOWN_CORNER: UP_CORNER}

    def landing(s, kind):
        if kind in (LEFT, RIGHT):
            return rs.at[s, kind]
        if kind in (UP, DOWN):
            return vt.at[s, kind - UP]
        return cr.at[s, kind - UP_CORNER]

    def source(s, kind):
        if kind in (LEFT, RIGHT):
            return pk.at[s, kind]
        if kind in (UP, DOWN):
            return obj.at[s, :, (kind - UP) * HALF : (kind - UP + 1) * HALF]
        return rs.at[s, :, :, (kind - UP_CORNER) * BLOCK : (kind - UP_CORNER + 1) * BLOCK]

    def halo_copy(s, kind):
        return pltpu.make_async_remote_copy(
            src_ref=source(s, kind),
            dst_ref=landing(s, opposite[kind]),
            send_sem=halo_send.at[s, kind],
            recv_sem=halo_recv.at[s, opposite[kind]],
            device_id=target[kind if kind < UP_CORNER else kind - 2],
            device_id_type=MESH,
        )

    def start_halo(s, kind):
        @pl.when(has[kind])
        def _():
            halo_copy(s, kind).start()

    def await_halo(s, kind):
        @pl.when(has[kind])
        def _():
            halo_copy(s, opposite[kind]).wait_recv()

    for s in range(SLICES):
        for kind in (LEFT, RIGHT, UP, DOWN):
            start_halo(s, kind)

    def relay_corners(s):
        await_halo(s, LEFT)
        await_halo(s, RIGHT)
        start_halo(s, UP_CORNER)
        start_halo(s, DOWN_CORNER)

    row, col = pos_ref[0], pos_ref[1]
    here, there = (lax.broadcasted_iota(jnp.int32, (DET, 2 * DET), d) for d in range(2))
    pick_rows = jnp.where(there == here + row, 1.0, 0.0).astype(BF16)
    offset = here + (col + 2 * DET - HALF)
    offset = jnp.where(offset >= 2 * DET, offset - 2 * DET, offset)
    pick_cols = jnp.where(there == offset, 1.0, 0.0).astype(BF16)
    here, there = (lax.broadcasted_iota(jnp.int32, (2 * DET, DET), d) for d in range(2))
    put_rows = jnp.where(here == there + row, 1.0, 0.0).astype(BF16)
    offset = there + (col + 2 * DET - HALF)
    offset = jnp.where(offset >= 2 * DET, offset - 2 * DET, offset)
    put_cols = jnp.where(here == offset, 1.0, 0.0).astype(BF16)

    def twice(x, axis):
        return jnp.concatenate([x, x], axis=axis)

    def both(x, axis):
        return jnp.concatenate(halves(x), axis=axis)

    def dot(x, y):
        return jnp.dot(x, y, preferred_element_type=F32)

    def build_window(s):
        for kind in (UP, DOWN, UP_CORNER, DOWN_CORNER):
            await_halo(s, kind)
        for c in range(2):
            for side in range(2):
                at = side * 3 * HALF
                ext[c, at : at + HALF, :DET] = vt[s, side, c]
                first, second = unpacked_sides(cr[s, side, LEFT, c], cr[s, side, RIGHT, c])
                ext[c, at : at + BLOCK, DET:] = first
                ext[c, at + BLOCK : at + HALF, DET:] = second
            ext[c, HALF : 3 * HALF, :DET] = obj[s, c]
            for b in range(2):
                block = slice(b * BLOCK, (b + 1) * BLOCK)
                first, second = unpacked_sides(rs[s, LEFT, c, block], rs[s, RIGHT, c, block])
                at = HALF + b * HALF
                ext[c, at : at + BLOCK, DET:] = first
                ext[c, at + BLOCK : at + HALF, DET:] = second
            band = dot(twice(pick_rows, 1), both(ext[c], 0))
            window[s, c] = dot(both(band, 1), twice(put_cols, 0))

    relay_corners(0)
    for s in range(SLICES):
        if s + 1 < SLICES:
            relay_corners(s + 1)
        build_window(s)

        def fetch(m):
            if s == 0:
                real, imag = probe[m, 0], probe[m, 1]
            else:
                real, imag = psi[s - 1, 0, rows(m)], psi[s - 1, 1, rows(m)]
            wr, wi = window[s, 0], window[s, 1]
            return real * wr - imag * wi, real * wi + imag * wr

        def deliver(m, real, imag):
            if s + 1 < SLICES:
                psi[s, 0, rows(m)] = real
                psi[s, 1, rows(m)] = imag
            else:
                far[0, rows(m)] = real
                far[1, rows(m)] = imag
                power = real * real + imag * imag
                part[...] = power if m == 0 else part[...] + power

        two_sided(mats, STEP if s + 1 < SLICES else FAR, fetch, deliver, mid)

    def mode_copy(step):
        return pltpu.make_async_remote_copy(
            src_ref=part,
            dst_ref=others.at[step - 1],
            send_sem=mode_send.at[step - 1],
            recv_sem=mode_recv.at[step - 1],
            device_id=peer(step),
            device_id_type=MESH,
        )

    for step in range(1, modes):
        mode_copy(step).start()
    whole = part[...]
    for step in range(1, modes):
        mode_copy(step).wait_recv()
        whole = whole + others[step - 1]
    weight = 1.0 - measured[0, 0, 0] / jnp.maximum(jnp.sqrt(whole), 1.0)

    def term_copy(s):
        slot = lax.rem(s - mode + modes, modes) - 1
        return pltpu.make_async_remote_copy(
            src_ref=term.at[s],
            dst_ref=parts.at[slot],
            send_sem=term_send.at[s],
            recv_sem=term_recv.at[slot],
            device_id={"mode": s, "ty": ty, "tx": tx},
            device_id_type=MESH,
        )

    for s in reversed(range(SLICES)):

        def fetch(m):
            if s == SLICES - 1:
                return weight * far[0, rows(m)], weight * far[1, rows(m)]
            return pulled[0, rows(m)], pulled[1, rows(m)]

        def deliver(m, real, imag):
            if s == 0:
                pr, pi = probe[m, 0], probe[m, 1]
            else:
                pr, pi = psi[s - 1, 0, rows(m)], psi[s - 1, 1, rows(m)]
            tr, ti = pr * real + pi * imag, pr * imag - pi * real
            term[s, 0] = tr if m == 0 else term[s, 0] + tr
            term[s, 1] = ti if m == 0 else term[s, 1] + ti
            if s > 0:
                wr, wi = window[s, 0], window[s, 1]
                pulled[0, rows(m)] = wr * real + wi * imag
                pulled[1, rows(m)] = wr * imag - wi * real

        two_sided(mats, FAR_BACK if s == SLICES - 1 else STEP_BACK, fetch, deliver, mid)

        @pl.when(mode != s)
        def _():
            term_copy(s).start()

    for step in range(1, modes):
        pltpu.make_async_remote_copy(
            src_ref=term.at[0],
            dst_ref=parts.at[step - 1],
            send_sem=term_send.at[0],
            recv_sem=term_recv.at[step - 1],
            device_id=peer(step),
            device_id_type=MESH,
        ).wait_recv()

    for c in range(2):
        mine = term[mode, c]
        for step in range(1, modes):
            mine = mine + parts[step - 1, c]
        tall = dot(twice(put_rows, 1), both(mine, 0))
        grid[c] = dot(both(tall, 1), twice(pick_cols, 0))

    def grad_copy(kind):
        if kind in (UP, DOWN):
            at = (kind - UP) * 3 * HALF
            src, dst = grid.at[:, at : at + HALF], gv.at[opposite[kind] - UP]
            where = target[kind]
        else:
            src, dst = hp.at[kind], gh.at[opposite[kind]]
            where = direct[kind]
        return pltpu.make_async_remote_copy(
            src_ref=src,
            dst_ref=dst,
            send_sem=grad_send.at[kind],
            recv_sem=grad_recv.at[opposite[kind]],
            device_id=where,
            device_id_type=MESH,
        )

    def exchange(kinds):
        for kind in kinds:

            @pl.when(has[kind])
            def _():
                grad_copy(kind).start()

        for kind in kinds:

            @pl.when(has[kind])
            def _():
                grad_copy(opposite[kind]).wait_recv()

    exchange((UP, DOWN))
    for c in range(2):
        for b in range(2):
            block = slice(b * HALF, (b + 1) * HALF)
            middle[c, block] = grid[c, HALF + b * HALF : 2 * HALF + b * HALF] + gv[b, c]
        upper, lower = middle[c, :HALF, DET:], middle[c, HALF:, DET:]
        low = lane_low(upper.shape)
        hp[RIGHT, c] = jnp.where(low, upper, turned(lower))
        hp[LEFT, c] = jnp.where(low, turned(upper), lower)
    exchange((LEFT, RIGHT))
    for c in range(2):
        low = lane_low(gh[LEFT, c].shape)
        out[0, c, :HALF] = middle[c, :HALF, :DET] + jnp.where(low, gh[LEFT, c], turned(gh[RIGHT, c]))
        out[0, c, HALF:] = middle[c, HALF:, :DET] + jnp.where(low, turned(gh[LEFT, c]), gh[RIGHT, c])

    for kind in range(6):

        @pl.when(has[kind])
        def _():
            for s in range(SLICES):
                halo_copy(s, kind).wait_send()
            if kind < UP_CORNER:
                grad_copy(kind).wait_send()

    for step in range(1, modes):
        mode_copy(step).wait_send()
    for s in range(SLICES):

        @pl.when(mode != s)
        def _():
            term_copy(s).wait_send()


VMEM = pl.BlockSpec(memory_space=pltpu.VMEM)
SMEM = pl.BlockSpec(memory_space=pltpu.SMEM)


def body(object_slices, probe_modes, positions, measured):
    mats = jnp.asarray(tables())
    modes = lax.axis_size("mode")
    dma = pltpu.SemaphoreType.DMA
    wave = (LOCAL * DET, DET)
    scratch = dict(
        pk=(SLICES, 2, 2, HALF, DET),
        rs=(SLICES, 2, 2, HALF, DET),
        vt=(SLICES, 2, 2, HALF, DET),
        cr=(SLICES, 2, 2, 2, BLOCK, DET),
        ext=(2, 2 * DET, 2 * DET),
        window=(SLICES, 2, DET, DET),
        psi=(SLICES - 1, 2, *wave),
        far=(2, *wave),
        part=(DET, DET),
        others=(modes - 1, DET, DET),
        mid=(4 * DET, LOCAL * DET),
        pulled=(2, *wave),
        term=(SLICES, 2, DET, DET),
        parts=(modes - 1, 2, DET, DET),
        grid=(2, 2 * DET, 2 * DET),
        gv=(2, 2, HALF, 2 * DET),
        middle=(2, DET, 2 * DET),
        hp=(2, 2, HALF, DET),
        gh=(2, 2, HALF, DET),
    )
    return pl.pallas_call(
        kernel,
        out_shape=jax.ShapeDtypeStruct((1, 2, DET, DET), F32),
        in_specs=[SMEM, VMEM, VMEM, VMEM, VMEM],
        out_specs=VMEM,
        scratch_shapes=[pltpu.VMEM(shape, BF16 if name == "mid" else F32) for name, shape in scratch.items()]
        + [dma((SLICES, 6)), dma((SLICES, 6))]
        + [dma((modes - 1,)), dma((modes - 1,))]
        + [dma((SLICES,)), dma((modes - 1,))]
        + [dma((4,)), dma((4,))],
        compiler_params=pltpu.CompilerParams(collective_id=0, has_side_effects=True),
        name="ptycho",
    )(positions.reshape(2), object_slices, probe_modes, measured, mats)


def solution(mesh):
    return jax.shard_map(
        body,
        mesh=mesh,
        in_specs=(
            P(None, None, "ty", "tx"),
            P("mode", None, None, None),
            P("ty", "tx", None, None),
            P("ty", "tx", None, None, None),
        ),
        out_specs=P("mode", None, "ty", "tx"),
        check_vma=False,
    )
```

time: 130 us -> 63.6 us (0.49)
  Pallas kernels: 11.4 us -> 61.9 us
  waiting for transfers between devices: 42.5 us -> 0 us
  starting transfers between devices: 33.7 us -> 0 us
  blocking collectives: 22.3 us -> 0 us
  local copies, waits for them, and re-layouts: 12 us -> 1.57 us
  between operations: 4.03 us -> 0.01 us
  other arithmetic: 3.14 us -> 0 us
    pallas_call x2 -> x1, Pallas kernels: 11.4 us -> 61.9 us  [body(): pl.pallas_call(kernel, out_shape=jax.ShapeDtypeStruct((1, 2, DET, DET), F...]
    ppermute x8 -> x0, waiting for transfers between devices: 32.9 us -> none  [the longest x2 13.3 us: extended(): after = lax.ppermute(leading, axis, down)]
    ppermute x8 -> x0, starting transfers between devices: 30.2 us -> none  [the longest x4 13.9 us: shifted(): return lax.ppermute(block, axis, route)]
    all_to_all x1 -> x0, blocking collectives: 22.3 us -> none  [body(): lax.all_to_all(copies, 'mode', split_axis=0, concat_axis=0, tiled=True)]
    all_to_all x1 -> x0, waiting for transfers between devices: 9.62 us -> none  [body(): lax.all_to_all(terms, 'mode', split_axis=0, concat_axis=0, tiled=True)]
    slice x9 -> x0, local copies, waits for them, and re-layouts: 3.65 us -> none  [the longest x2 1.47 us: extended(): last = lax.slice_in_dim(shard, length - width, length, axis=dim)]
    all_to_all x1 -> x0, starting transfers between devices: 3.47 us -> none  [body(): lax.all_to_all(terms, 'mode', split_axis=0, concat_axis=0, tiled=True)]
    dynamic_update_slice x1 -> x0, local copies, waits for them, and re-layouts: 2.42 us -> none  [body(): gradient = lax.dynamic_update_slice(gradient, mine, (0, 0, pos[0], pos[1]))]
  transfers between devices with their start and end apart: 9 -> 0, of which waited for: 8 -> 0; matrix products, arithmetic and copies ran while one was open for 2% -> 0% of each run, Pallas kernels for 0% -> 0%
where the time goes in v1:
time: 63.6 us; the launch traced here: 63.5 us
  Pallas kernels  61.9 us (97%)
  local copies, waits for them, and re-layouts  1.57 us (2%)
    pallas_call x1, Pallas kernels, body(): pl.pallas_call(kernel, out_shape=jax.ShapeDtypeStruct((1, 2, DET, DET), F...  61.9 us
    unnamed x1, local copies, waits for them, and re-layouts  1.57 us

profile of v1, /device:TPU:7, one launch (start us, length us, event | category | flops | bytes accessed | tf_op | source)
XLA Modules:
  0.0 63.5 jit_solution(17691704383808635331)
XLA Ops:
  0.0 61.9 %ptycho.1 = f32[1,2,128,128]{3,2,1,0:T(8,128)} custom-call(s32[2]{0:T(128)} %bitcast.1, f32[4,2,128,128]{3,2,1,0:T(8,128)} %obj.1, f32[4,2,128,128]{3,2,1,0:T(8,128)} %probe.1, f32[1,1,1,128,128]{4,3,2,1,0:T(8,128)} %measured.1, bf16[8,256,256]{2,1,0:T(8,128)(2,1)} %constant.2.clone.mats), custom_call_target="tpu_custom_call" | custom-call | tf_op jit(solution)/shard_map/ptycho/pallas_call | solution.py:460
  61.9 1.6 %copy.7 = f32[1,2,128,128]{3,2,1,0:T(8,128)} copy(f32[1,2,128,128]{3,2,1,0:T(8,128)} %ptycho.1) | data formatting | bytes 262144

commit v2 on v1

--- a/solution.py
+++ b/solution.py
@@ -62,9 +62,9 @@
 def left_product(mats, which, stacked):
     conj = CONJ[which]
     high, low = mats[2 * conj], mats[2 * conj + 1]
-    lhs = jnp.concatenate([high, high, low], axis=1)
-    rhs = jnp.concatenate([stacked, stacked[: 2 * DET]], axis=0)
-    return jnp.dot(lhs, rhs, preferred_element_type=F32)
+    main = jnp.dot(jnp.concatenate([high, low], axis=0), stacked[: 2 * DET], preferred_element_type=F32)
+    rest = jnp.dot(high, stacked[2 * DET :], preferred_element_type=F32)
+    return main[: 2 * DET] + main[2 * DET :] + rest
 
 
 def two_sided(mats, which, fetch, deliver, mid):
@@ -80,7 +80,6 @@
         for k in range(2):
             deliver(2 * pair + k, out[:DET, rows(k)], out[DET:, rows(k)])
 
-
 MESH = pl.DeviceIdType.MESH
 HALF = DET // 2
 BLOCK = HALF // 2
@@ -113,9 +112,9 @@
 
 
 def kernel(
-    pos_ref, obj, probe, measured, mats, out,
-    pk, rs, vt, cr, ext, window, psi, far, part, others, mid, pulled, term, parts, grid, gv, middle, hp, gh,
-    halo_send, halo_recv, mode_send, mode_recv, term_send, term_recv, grad_send, grad_recv,
+    pos_ref, obj, probe_in, measured_in, mats_in, out,
+    probe, measured, mats, pk, rs, rl, vt, cr, ext, window, psi, far, part, others, mid, pulled, term, parts, grid, gv, middle, hp, gh,
+    load, halo_send, halo_recv, cross_send, cross_recv, relay_send, relay_recv, mode_send, mode_recv, term_send, term_recv, grad_send, grad_recv,
 ):
     mode, ty, tx = lax.axis_index("mode"), lax.axis_index("ty"), lax.axis_index("tx")
     modes, tys, txs = lax.axis_size("mode"), lax.axis_size("ty"), lax.axis_size("tx")
@@ -131,10 +130,18 @@
         UP: {"mode": mode, "ty": ty - 1, "tx": tx},
         DOWN: {"mode": mode, "ty": ty + 1, "tx": tx},
     }
+    crossing = {LEFT: cross_left, RIGHT: cross_right}
+    relay_tx = {LEFT: 0, RIGHT: txs - 1}
+    relaying = {LEFT: tx == relay_tx[LEFT], RIGHT: tx == relay_tx[RIGHT]}
+    landing_tx = {LEFT: txs // 2 - 1, RIGHT: txs // 2}
     direct = {LEFT: {"mode": mode, "ty": ty, "tx": tx - 1}, RIGHT: {"mode": mode, "ty": ty, "tx": tx + 1}}
 
     def peer(step):
         return {"mode": lax.rem(mode + step, modes), "ty": ty, "tx": tx}
+
+    loads = [pltpu.make_async_copy(src, dst, load.at[i]) for i, (src, dst) in enumerate(((probe_in, probe), (mats_in, mats), (measured_in, measured)))]
+    for copy in loads:
+        copy.start()
 
     for side in (LEFT, RIGHT):
 
@@ -175,6 +182,20 @@
         def _():
             pl.semaphore_signal(barrier, inc=1, device_id=direct[side], device_id_type=MESH)
 
+    for side in (LEFT, RIGHT):
+        from_relay, from_landing = crossing[side], relaying[side]
+        count = count + from_relay.astype(jnp.int32) + from_landing.astype(jnp.int32)
+
+        @pl.when(relaying[side])
+        def _():
+            sender = {"mode": mirror, "ty": ty, "tx": landing_tx[1 - side]}
+            pl.semaphore_signal(barrier, inc=1, device_id=sender, device_id_type=MESH)
+
+        @pl.when(tx == landing_tx[side])
+        def _():
+            relay = {"mode": mode, "ty": ty, "tx": relay_tx[side]}
+            pl.semaphore_signal(barrier, inc=1, device_id=relay, device_id_type=MESH)
+
     for step in range(1, modes):
         pl.semaphore_signal(barrier, inc=1, device_id=peer(step), device_id_type=MESH)
     pl.semaphore_wait(barrier, count)
@@ -205,15 +226,70 @@
             device_id_type=MESH,
         )
 
+    def straight_copy(s, kind):
+        return pltpu.make_async_remote_copy(
+            src_ref=pk.at[s, kind, 0],
+            dst_ref=rs.at[s, opposite[kind], 0],
+            send_sem=cross_send.at[s, 0],
+            recv_sem=cross_recv.at[s, 0],
+            device_id=target[kind],
+            device_id_type=MESH,
+        )
+
+    def detour_copy(s, kind):
+        return pltpu.make_async_remote_copy(
+            src_ref=pk.at[s, kind, 1],
+            dst_ref=rl.at[s],
+            send_sem=cross_send.at[s, 1],
+            recv_sem=relay_recv.at[s],
+            device_id={"mode": mirror, "ty": ty, "tx": relay_tx[kind]},
+            device_id_type=MESH,
+        )
+
+    def onward_copy(s, kind):
+        return pltpu.make_async_remote_copy(
+            src_ref=rl.at[s],
+            dst_ref=rs.at[s, opposite[kind], 1],
+            send_sem=relay_send.at[s],
+            recv_sem=cross_recv.at[s, 1],
+            device_id={"mode": mode, "ty": ty, "tx": landing_tx[kind]},
+            device_id_type=MESH,
+        )
+
+    def near(kind):
+        return jnp.logical_and(has[kind], jnp.logical_not(crossing[kind])) if kind in crossing else has[kind]
+
     def start_halo(s, kind):
-        @pl.when(has[kind])
+        @pl.when(near(kind))
         def _():
             halo_copy(s, kind).start()
 
+        if kind in crossing:
+
+            @pl.when(crossing[kind])
+            def _():
+                straight_copy(s, kind).start()
+                detour_copy(s, kind).start()
+
     def await_halo(s, kind):
-        @pl.when(has[kind])
+        @pl.when(near(kind))
         def _():
             halo_copy(s, opposite[kind]).wait_recv()
+
+        if kind in crossing:
+
+            @pl.when(crossing[kind])
+            def _():
+                straight_copy(s, opposite[kind]).wait_recv()
+                onward_copy(s, opposite[kind]).wait_recv()
+
+    def relay(s):
+        for kind in (LEFT, RIGHT):
+
+            @pl.when(relaying[kind])
+            def _():
+                detour_copy(s, kind).wait_recv()
+                onward_copy(s, kind).start()
 
     for s in range(SLICES):
         for kind in (LEFT, RIGHT, UP, DOWN):
@@ -267,10 +343,17 @@
             window[s, c] = dot(both(band, 1), twice(put_cols, 0))
 
     relay_corners(0)
+    relay(0)
     for s in range(SLICES):
         if s + 1 < SLICES:
             relay_corners(s + 1)
+        for ahead in range(2 * s, min(2 * s + 2, SLICES)):
+            if ahead:
+                relay(ahead)
         build_window(s)
+        if s == 0:
+            for copy in loads:
+                copy.wait()
 
         def fetch(m):
             if s == 0:
@@ -411,12 +494,29 @@
 
     for kind in range(6):
 
-        @pl.when(has[kind])
+        @pl.when(near(kind))
         def _():
             for s in range(SLICES):
                 halo_copy(s, kind).wait_send()
-            if kind < UP_CORNER:
+
+        if kind < UP_CORNER:
+
+            @pl.when(has[kind])
+            def _():
                 grad_copy(kind).wait_send()
+
+    for kind in (LEFT, RIGHT):
+
+        @pl.when(crossing[kind])
+        def _():
+            for s in range(SLICES):
+                straight_copy(s, kind).wait_send()
+                detour_copy(s, kind).wait_send()
+
+        @pl.when(relaying[kind])
+        def _():
+            for s in range(SLICES):
+                onward_copy(s, kind).wait_send()
 
     for step in range(1, modes):
         mode_copy(step).wait_send()
@@ -429,6 +529,7 @@
 
 VMEM = pl.BlockSpec(memory_space=pltpu.VMEM)
 SMEM = pl.BlockSpec(memory_space=pltpu.SMEM)
+ANY = pl.BlockSpec(memory_space=pl.ANY)
 
 
 def body(object_slices, probe_modes, positions, measured):
@@ -437,8 +538,12 @@
     dma = pltpu.SemaphoreType.DMA
     wave = (LOCAL * DET, DET)
     scratch = dict(
+        probe=(LOCAL, 2, DET, DET),
+        measured=(1, 1, 1, DET, DET),
+        mats=(8, 2 * DET, 2 * DET),
         pk=(SLICES, 2, 2, HALF, DET),
         rs=(SLICES, 2, 2, HALF, DET),
+        rl=(SLICES, HALF, DET),
         vt=(SLICES, 2, 2, HALF, DET),
         cr=(SLICES, 2, 2, 2, BLOCK, DET),
         ext=(2, 2 * DET, 2 * DET),
@@ -460,10 +565,12 @@
     return pl.pallas_call(
         kernel,
         out_shape=jax.ShapeDtypeStruct((1, 2, DET, DET), F32),
-        in_specs=[SMEM, VMEM, VMEM, VMEM, VMEM],
+        in_specs=[SMEM, VMEM, ANY, ANY, ANY],
         out_specs=VMEM,
-        scratch_shapes=[pltpu.VMEM(shape, BF16 if name == "mid" else F32) for name, shape in scratch.items()]
+        scratch_shapes=[pltpu.VMEM(shape, BF16 if name in ("mid", "mats") else F32) for name, shape in scratch.items()]
+        + [dma((3,))]
         + [dma((SLICES, 6)), dma((SLICES, 6))]
+        + [dma((SLICES, 2)), dma((SLICES, 2)), dma((SLICES,)), dma((SLICES,))]
         + [dma((modes - 1,)), dma((modes - 1,))]
         + [dma((SLICES,)), dma((modes - 1,))]
         + [dma((4,)), dma((4,))],

time: 63.6 us -> 65.9 us (1.036)
  Pallas kernels: 61.9 us -> 63.5 us
    pallas_call x1, Pallas kernels: 61.9 us -> 63.5 us  [body(): pl.pallas_call(kernel, out_shape=jax.ShapeDtypeStruct((1, 2, DET, DET), F...]
where the time goes in v2:
time: 65.9 us; the launch traced here: 65.1 us
  Pallas kernels  63.5 us (96%)
  local copies, waits for them, and re-layouts  1.57 us (2%)
    pallas_call x1, Pallas kernels, body(): pl.pallas_call(kernel, out_shape=jax.ShapeDtypeStruct((1, 2, DET, DET), F...  63.5 us
    unnamed x1, local copies, waits for them, and re-layouts  1.57 us

profile of v2, /device:TPU:7, one launch (start us, length us, event | category | flops | bytes accessed | tf_op | source)
XLA Modules:
  0.0 65.1 jit_solution(8890487363673987628)
XLA Ops:
  0.0 63.5 %ptycho.1 = f32[1,2,128,128]{3,2,1,0:T(8,128)} custom-call(s32[2]{0:T(128)} %bitcast.1, f32[4,2,128,128]{3,2,1,0:T(8,128)} %obj.1, f32[4,2,128,128]{3,2,1,0:T(8,128)} %probe_in.1, f32[1,1,1,128,128]{4,3,2,1,0:T(8,128)} %measured_in.1, bf16[8,256,256]{2,1,0:T(8,128)(2,1)} %constant.2.clone.mats_in), custom_call_target="tpu_custom_call" | custom-call | tf_op jit(solution)/shard_map/ptycho/pallas_call | solution.py:565
  63.5 1.6 %copy.7 = f32[1,2,128,128]{3,2,1,0:T(8,128)} copy(f32[1,2,128,128]{3,2,1,0:T(8,128)} %ptycho.1) | data formatting | bytes 262144

commit v3 on v2

--- a/solution.py
+++ b/solution.py
@@ -131,7 +131,7 @@
         DOWN: {"mode": mode, "ty": ty + 1, "tx": tx},
     }
     crossing = {LEFT: cross_left, RIGHT: cross_right}
-    relay_tx = {LEFT: 0, RIGHT: txs - 1}
+    relay_tx = {LEFT: txs - 1, RIGHT: 0}
     relaying = {LEFT: tx == relay_tx[LEFT], RIGHT: tx == relay_tx[RIGHT]}
     landing_tx = {LEFT: txs // 2 - 1, RIGHT: txs // 2}
     direct = {LEFT: {"mode": mode, "ty": ty, "tx": tx - 1}, RIGHT: {"mode": mode, "ty": ty, "tx": tx + 1}}
@@ -188,12 +188,12 @@
 
         @pl.when(relaying[side])
         def _():
-            sender = {"mode": mirror, "ty": ty, "tx": landing_tx[1 - side]}
+            sender = {"mode": mode, "ty": ty, "tx": landing_tx[1 - side]}
             pl.semaphore_signal(barrier, inc=1, device_id=sender, device_id_type=MESH)
 
         @pl.when(tx == landing_tx[side])
         def _():
-            relay = {"mode": mode, "ty": ty, "tx": relay_tx[side]}
+            relay = {"mode": mirror, "ty": ty, "tx": relay_tx[side]}
             pl.semaphore_signal(barrier, inc=1, device_id=relay, device_id_type=MESH)
 
     for step in range(1, modes):
@@ -242,7 +242,7 @@
             dst_ref=rl.at[s],
             send_sem=cross_send.at[s, 1],
             recv_sem=relay_recv.at[s],
-            device_id={"mode": mirror, "ty": ty, "tx": relay_tx[kind]},
+            device_id={"mode": mode, "ty": ty, "tx": relay_tx[kind]},
             device_id_type=MESH,
         )
 
@@ -252,7 +252,7 @@
             dst_ref=rs.at[s, opposite[kind], 1],
             send_sem=relay_send.at[s],
             recv_sem=cross_recv.at[s, 1],
-            device_id={"mode": mode, "ty": ty, "tx": landing_tx[kind]},
+            device_id={"mode": mirror, "ty": ty, "tx": landing_tx[kind]},
             device_id_type=MESH,
         )
 

time: 65.9 us -> 61.8 us (0.938)
  Pallas kernels: 63.5 us -> 59.6 us
    pallas_call x1, Pallas kernels: 63.5 us -> 59.6 us  [body(): pl.pallas_call(kernel, out_shape=jax.ShapeDtypeStruct((1, 2, DET, DET), F...]
where the time goes in v3:
time: 61.8 us; the launch traced here: 61.2 us
  Pallas kernels  59.6 us (96%)
  local copies, waits for them, and re-layouts  1.57 us (3%)
    pallas_call x1, Pallas kernels, body(): pl.pallas_call(kernel, out_shape=jax.ShapeDtypeStruct((1, 2, DET, DET), F...  59.6 us
    unnamed x1, local copies, waits for them, and re-layouts  1.57 us

profile of v3, /device:TPU:7, one launch (start us, length us, event | category | flops | bytes accessed | tf_op | source)
XLA Modules:
  0.0 61.2 jit_solution(6267905594690074534)
XLA Ops:
  0.0 59.6 %ptycho.1 = f32[1,2,128,128]{3,2,1,0:T(8,128)} custom-call(s32[2]{0:T(128)} %bitcast.1, f32[4,2,128,128]{3,2,1,0:T(8,128)} %obj.1, f32[4,2,128,128]{3,2,1,0:T(8,128)} %probe_in.1, f32[1,1,1,128,128]{4,3,2,1,0:T(8,128)} %measured_in.1, bf16[8,256,256]{2,1,0:T(8,128)(2,1)} %constant.2.clone.mats_in), custom_call_target="tpu_custom_call" | custom-call | tf_op jit(solution)/shard_map/ptycho/pallas_call | solution.py:565
  59.6 1.6 %copy.7 = f32[1,2,128,128]{3,2,1,0:T(8,128)} copy(f32[1,2,128,128]{3,2,1,0:T(8,128)} %ptycho.1) | data formatting | bytes 262144

commit v4 on v3

--- a/solution.py
+++ b/solution.py
@@ -108,13 +108,25 @@
     return first, second
 
 
+def packed_sides(strip):
+    half = strip.shape[0] // 2
+    upper, lower = strip[:half], strip[half:]
+    low = lane_low(upper.shape)
+    return jnp.where(low, turned(upper), lower), jnp.where(low, upper, turned(lower))
+
+
+def unpacked_halves(from_left, from_right):
+    low = lane_low(from_left.shape)
+    return jnp.where(low, from_left, turned(from_right)), jnp.where(low, turned(from_left), from_right)
+
+
 LEFT, RIGHT, UP, DOWN, UP_CORNER, DOWN_CORNER = range(6)
 
 
 def kernel(
     pos_ref, obj, probe_in, measured_in, mats_in, out,
-    probe, measured, mats, pk, rs, rl, vt, cr, ext, window, psi, far, part, others, mid, pulled, term, parts, grid, gv, middle, hp, gh,
-    load, halo_send, halo_recv, cross_send, cross_recv, relay_send, relay_recv, mode_send, mode_recv, term_send, term_recv, grad_send, grad_recv,
+    probe, measured, mats, pk, rs, rl, vt, cr, ext, window, psi, far, part, others, mid, pulled, term, collected, joint, parts, middle, vp, hp, cp, gv, gh, gc,
+    load, halo_send, halo_recv, cross_send, cross_recv, relay_send, relay_recv, mode_send, mode_recv, collect_send, collect_recv, joint_send, joint_recv, partner_send, partner_recv, grad_send, grad_recv,
 ):
     mode, ty, tx = lax.axis_index("mode"), lax.axis_index("ty"), lax.axis_index("tx")
     modes, tys, txs = lax.axis_size("mode"), lax.axis_size("ty"), lax.axis_size("tx")
@@ -149,6 +161,7 @@
         def _():
             rs[:, side] = jnp.zeros_like(rs[:, side])
             gh[side] = jnp.zeros_like(gh[side])
+            gc[:, side] = jnp.zeros_like(gc[:, side])
 
     for side in (UP, DOWN):
 
@@ -157,6 +170,7 @@
             vt[:, side - UP] = jnp.zeros_like(vt[:, side - UP])
             cr[:, side - UP] = jnp.zeros_like(cr[:, side - UP])
             gv[side - UP] = jnp.zeros_like(gv[side - UP])
+            gc[side - UP] = jnp.zeros_like(gc[side - UP])
 
     for s in range(SLICES):
         for c in range(2):
@@ -375,6 +389,9 @@
 
         two_sided(mats, STEP if s + 1 < SLICES else FAR, fetch, deliver, mid)
 
+    first, last = mode == 0, mode == modes - 1
+    inner, lower = jnp.logical_not(jnp.logical_or(first, last)), mode < modes // 2
+
     def mode_copy(step):
         return pltpu.make_async_remote_copy(
             src_ref=part,
@@ -393,16 +410,62 @@
         whole = whole + others[step - 1]
     weight = 1.0 - measured[0, 0, 0] / jnp.maximum(jnp.sqrt(whole), 1.0)
 
-    def term_copy(s):
-        slot = lax.rem(s - mode + modes, modes) - 1
-        return pltpu.make_async_remote_copy(
-            src_ref=term.at[s],
-            dst_ref=parts.at[slot],
-            send_sem=term_send.at[s],
-            recv_sem=term_recv.at[slot],
-            device_id={"mode": s, "ty": ty, "tx": tx},
-            device_id_type=MESH,
-        )
+    outer, collector = jnp.logical_or(first, last), jnp.where(lower, 1, 2)
+
+    def far_slice(low_pair, i):
+        return SLICES - 1 - i if low_pair else 1 - i
+
+    def piece(q):
+        return q // 2, pl.ds(q % 2 * HALF, HALF)
+
+    def collect_copy(low_pair, i, q):
+        return pltpu.make_async_remote_copy(
+            src_ref=term.at[(far_slice(low_pair, i), *piece(q))],
+            dst_ref=collected.at[(i, *piece(q))],
+            send_sem=collect_send.at[i, q],
+            recv_sem=collect_recv.at[i, q],
+            device_id={"mode": collector, "ty": ty, "tx": tx},
+            device_id_type=MESH,
+        )
+
+    def pair_sum_copy(low_pair, i, q):
+        return pltpu.make_async_remote_copy(
+            src_ref=joint.at[(i, *piece(q))],
+            dst_ref=parts.at[(1, *piece(q))],
+            send_sem=joint_send.at[i, q],
+            recv_sem=joint_recv.at[q],
+            device_id={"mode": far_slice(low_pair, i), "ty": ty, "tx": tx},
+            device_id_type=MESH,
+        )
+
+    def partner_copy(owner):
+        return pltpu.make_async_remote_copy(
+            src_ref=term.at[owner],
+            dst_ref=parts.at[0],
+            send_sem=partner_send,
+            recv_sem=partner_recv,
+            device_id={"mode": owner, "ty": ty, "tx": tx},
+            device_id_type=MESH,
+        )
+
+    def send_far(low_pair, i):
+        @pl.when(first if low_pair else last)
+        def _():
+            for q in range(4):
+                collect_copy(low_pair, i, q).start()
+
+    def send_partner(owner):
+        @pl.when(mode == (owner ^ 1))
+        def _():
+            partner_copy(owner).start()
+
+    def join(low_pair, i):
+        s = far_slice(low_pair, i)
+        for q in range(4):
+            collect_copy(low_pair, i, q).wait_recv()
+            at = piece(q)
+            joint[(i, *at)] = collected[(i, *at)] + term[(s, *at)]
+            pair_sum_copy(low_pair, i, q).start()
 
     for s in reversed(range(SLICES)):
 
@@ -426,71 +489,86 @@
 
         two_sided(mats, FAR_BACK if s == SLICES - 1 else STEP_BACK, fetch, deliver, mid)
 
-        @pl.when(mode != s)
-        def _():
-            term_copy(s).start()
-
-    for step in range(1, modes):
-        pltpu.make_async_remote_copy(
-            src_ref=term.at[0],
-            dst_ref=parts.at[step - 1],
-            send_sem=term_send.at[0],
-            recv_sem=term_recv.at[step - 1],
-            device_id=peer(step),
-            device_id_type=MESH,
-        ).wait_recv()
-
+        if s == 3:
+            send_far(True, 0)
+            send_partner(3)
+        elif s == 2:
+            send_far(True, 1)
+        elif s == 1:
+            send_partner(1)
+        else:
+            send_far(False, 1)
+            send_partner(0)
+            send_far(False, 0)
+            send_partner(2)
+
+    for low_pair in (True, False):
+
+        @pl.when(mode == (1 if low_pair else 2))
+        def _():
+            join(low_pair, 0 if low_pair else 1)
+            join(low_pair, 1 if low_pair else 0)
+
+    partner_copy(0).wait_recv()
+    for q in range(4):
+        pair_sum_copy(True, 0, q).wait_recv()
     for c in range(2):
         mine = term[mode, c]
-        for step in range(1, modes):
-            mine = mine + parts[step - 1, c]
+        mine = mine + parts[0, c] + parts[1, c]
         tall = dot(twice(put_rows, 1), both(mine, 0))
-        grid[c] = dot(both(tall, 1), twice(pick_cols, 0))
-
-    def grad_copy(kind):
-        if kind in (UP, DOWN):
-            at = (kind - UP) * 3 * HALF
-            src, dst = grid.at[:, at : at + HALF], gv.at[opposite[kind] - UP]
-            where = target[kind]
+        placed = dot(both(tall, 1), twice(pick_cols, 0))
+        middle[c] = placed[HALF : 3 * HALF, :DET]
+        for v in range(2):
+            at = 3 * v * HALF
+            vp[v, c] = placed[at : at + HALF, :DET]
+            cp[v, LEFT, c], cp[v, RIGHT, c] = packed_sides(placed[at : at + HALF, DET:])
+        hp[LEFT, c], hp[RIGHT, c] = packed_sides(placed[HALF : 3 * HALF, DET:])
+
+    def grad_has(v, h):
+        if v is None:
+            return has[h]
+        return has[UP + v] if h is None else jnp.logical_and(has[UP + v], has[h])
+
+    def grad_copy(v, h):
+        if v is None:
+            src, dst, i = hp.at[h], gh.at[1 - h], h
+        elif h is None:
+            src, dst, i = vp.at[v], gv.at[1 - v], 2 + v
         else:
-            src, dst = hp.at[kind], gh.at[opposite[kind]]
-            where = direct[kind]
+            src, dst, i = cp.at[v, h], gc.at[1 - v, 1 - h], 4 + 2 * v + h
         return pltpu.make_async_remote_copy(
             src_ref=src,
             dst_ref=dst,
-            send_sem=grad_send.at[kind],
-            recv_sem=grad_recv.at[opposite[kind]],
-            device_id=where,
-            device_id_type=MESH,
-        )
-
-    def exchange(kinds):
-        for kind in kinds:
-
-            @pl.when(has[kind])
-            def _():
-                grad_copy(kind).start()
-
-        for kind in kinds:
-
-            @pl.when(has[kind])
-            def _():
-                grad_copy(opposite[kind]).wait_recv()
-
-    exchange((UP, DOWN))
+            send_sem=grad_send.at[i],
+            recv_sem=grad_recv.at[i],
+            device_id={"mode": mode, "ty": ty if v is None else ty + 2 * v - 1, "tx": tx if h is None else tx + 2 * h - 1},
+            device_id_type=MESH,
+        )
+
+    directions = [(None, 0), (None, 1), (0, 0), (0, 1), (1, 0), (1, 1), (0, None), (1, None)]
+    for v, h in directions:
+
+        @pl.when(grad_has(v, h))
+        def _():
+            grad_copy(v, h).start()
+
+    for v, h in reversed(directions):
+        @pl.when(grad_has(v, h))
+        def _():
+            grad_copy(v if v is None else 1 - v, h if h is None else 1 - h).wait_recv()
+
     for c in range(2):
-        for b in range(2):
-            block = slice(b * HALF, (b + 1) * HALF)
-            middle[c, block] = grid[c, HALF + b * HALF : 2 * HALF + b * HALF] + gv[b, c]
-        upper, lower = middle[c, :HALF, DET:], middle[c, HALF:, DET:]
-        low = lane_low(upper.shape)
-        hp[RIGHT, c] = jnp.where(low, upper, turned(lower))
-        hp[LEFT, c] = jnp.where(low, turned(upper), lower)
-    exchange((LEFT, RIGHT))
-    for c in range(2):
-        low = lane_low(gh[LEFT, c].shape)
-        out[0, c, :HALF] = middle[c, :HALF, :DET] + jnp.where(low, gh[LEFT, c], turned(gh[RIGHT, c]))
-        out[0, c, HALF:] = middle[c, HALF:, :DET] + jnp.where(low, turned(gh[LEFT, c]), gh[RIGHT, c])
+        for v in range(2):
+            half = slice(v * HALF, (v + 1) * HALF)
+            sides = unpacked_halves(gh[LEFT, c], gh[RIGHT, c])[v]
+            corners = jnp.concatenate(unpacked_halves(gc[v, LEFT, c], gc[v, RIGHT, c]), axis=0)
+            out[0, c, half] = middle[c, half] + gv[v, c] + (sides + corners)
+
+    for v, h in directions:
+
+        @pl.when(grad_has(v, h))
+        def _():
+            grad_copy(v, h).wait_send()
 
     for kind in range(6):
 
@@ -498,12 +576,6 @@
         def _():
             for s in range(SLICES):
                 halo_copy(s, kind).wait_send()
-
-        if kind < UP_CORNER:
-
-            @pl.when(has[kind])
-            def _():
-                grad_copy(kind).wait_send()
 
     for kind in (LEFT, RIGHT):
 
@@ -520,11 +592,18 @@
 
     for step in range(1, modes):
         mode_copy(step).wait_send()
-    for s in range(SLICES):
-
-        @pl.when(mode != s)
-        def _():
-            term_copy(s).wait_send()
+
+    partner_copy(0).wait_send()
+    for i in range(2):
+        for q in range(4):
+
+            @pl.when(outer)
+            def _():
+                collect_copy(True, i, q).wait_send()
+
+            @pl.when(inner)
+            def _():
+                pair_sum_copy(True, i, q).wait_send()
 
 
 VMEM = pl.BlockSpec(memory_space=pltpu.VMEM)
@@ -555,12 +634,16 @@
         mid=(4 * DET, LOCAL * DET),
         pulled=(2, *wave),
         term=(SLICES, 2, DET, DET),
-        parts=(modes - 1, 2, DET, DET),
-        grid=(2, 2 * DET, 2 * DET),
-        gv=(2, 2, HALF, 2 * DET),
-        middle=(2, DET, 2 * DET),
+        collected=(2, 2, DET, DET),
+        joint=(2, 2, DET, DET),
+        parts=(2, 2, DET, DET),
+        middle=(2, DET, DET),
+        vp=(2, 2, HALF, DET),
         hp=(2, 2, HALF, DET),
+        cp=(2, 2, 2, BLOCK, DET),
+        gv=(2, 2, HALF, DET),
         gh=(2, 2, HALF, DET),
+        gc=(2, 2, 2, BLOCK, DET),
     )
     return pl.pallas_call(
         kernel,
@@ -572,8 +655,8 @@
         + [dma((SLICES, 6)), dma((SLICES, 6))]
         + [dma((SLICES, 2)), dma((SLICES, 2)), dma((SLICES,)), dma((SLICES,))]
         + [dma((modes - 1,)), dma((modes - 1,))]
-        + [dma((SLICES,)), dma((modes - 1,))]
-        + [dma((4,)), dma((4,))],
+        + [dma((2, 4)), dma((2, 4)), dma((2, 4)), dma((4,)), dma, dma]
+        + [dma((8,)), dma((8,))],
         compiler_params=pltpu.CompilerParams(collective_id=0, has_side_effects=True),
         name="ptycho",
     )(positions.reshape(2), object_slices, probe_modes, measured, mats)

time: 61.8 us -> 60 us (0.971)
  the two profiles are of different devices: /device:TPU:7 before, /device:TPU:39 now
where the time goes in v4:
time: 60 us; the launch traced here: 59.9 us
  Pallas kernels  58.3 us (97%)
  local copies, waits for them, and re-layouts  1.57 us (3%)
    pallas_call x1, Pallas kernels, body(): pl.pallas_call(kernel, out_shape=jax.ShapeDtypeStruct((1, 2, DET, DET), F...  58.3 us
    unnamed x1, local copies, waits for them, and re-layouts  1.57 us

profile of v4, /device:TPU:39, one launch (start us, length us, event | category | flops | bytes accessed | tf_op | source)
XLA Modules:
  0.0 59.9 jit_solution(13822419832181343388)
XLA Ops:
  0.0 58.3 %ptycho.1 = f32[1,2,128,128]{3,2,1,0:T(8,128)} custom-call(s32[2]{0:T(128)} %bitcast.1, f32[4,2,128,128]{3,2,1,0:T(8,128)} %obj.1, f32[4,2,128,128]{3,2,1,0:T(8,128)} %probe_in.1, f32[1,1,1,128,128]{4,3,2,1,0:T(8,128)} %measured_in.1, bf16[8,256,256]{2,1,0:T(8,128)(2,1)} %constant.2.clone.mats_in), custom_call_target="tpu_custom_call" | custom-call | tf_op jit(solution)/shard_map/ptycho/pallas_call | solution.py:648
  58.3 1.6 %copy.7 = f32[1,2,128,128]{3,2,1,0:T(8,128)} copy(f32[1,2,128,128]{3,2,1,0:T(8,128)} %ptycho.1) | data formatting | bytes 262144

commit v5 on v4

--- a/solution.py
+++ b/solution.py
@@ -83,6 +83,8 @@
 MESH = pl.DeviceIdType.MESH
 HALF = DET // 2
 BLOCK = HALF // 2
+EXTRA = 8
+STRAIGHT = ((0, slice(0, HALF)), (1, slice(0, EXTRA)))
 
 
 def lane_low(shape):
@@ -124,8 +126,8 @@
 
 
 def kernel(
-    pos_ref, obj, probe_in, measured_in, mats_in, out,
-    probe, measured, mats, pk, rs, rl, vt, cr, ext, window, psi, far, part, others, mid, pulled, term, collected, joint, parts, middle, vp, hp, cp, gv, gh, gc,
+    pos_ref, obj_in, probe_in, measured_in, mats_in, out,
+    obj, probe, measured, mats, pk, rs, rl, vt, cr, ext, window, psi, far, part, others, mid, pulled, term, collected, joint, parts, middle, vp, hp, cp, gv, gh, gc,
     load, halo_send, halo_recv, cross_send, cross_recv, relay_send, relay_recv, mode_send, mode_recv, collect_send, collect_recv, joint_send, joint_recv, partner_send, partner_recv, grad_send, grad_recv,
 ):
     mode, ty, tx = lax.axis_index("mode"), lax.axis_index("ty"), lax.axis_index("tx")
@@ -151,8 +153,42 @@
     def peer(step):
         return {"mode": lax.rem(mode + step, modes), "ty": ty, "tx": tx}
 
+    barrier = pltpu.get_barrier_semaphore()
+    count = jnp.int32(modes - 1)
+    for side in (LEFT, RIGHT, UP, DOWN):
+        count = count + has[side].astype(jnp.int32)
+
+        @pl.when(has[side])
+        def _():
+            pl.semaphore_signal(barrier, inc=1, device_id=target[side], device_id_type=MESH)
+
+    for side, cross in ((LEFT, cross_left), (RIGHT, cross_right)):
+        far_pair = jnp.logical_and(cross, has[side])
+        count = count + far_pair.astype(jnp.int32)
+
+        @pl.when(far_pair)
+        def _():
+            pl.semaphore_signal(barrier, inc=1, device_id=direct[side], device_id_type=MESH)
+
+    for side in (LEFT, RIGHT):
+        from_relay, from_landing = crossing[side], relaying[side]
+        count = count + from_relay.astype(jnp.int32) + from_landing.astype(jnp.int32)
+
+        @pl.when(relaying[side])
+        def _():
+            sender = {"mode": mode, "ty": ty, "tx": landing_tx[1 - side]}
+            pl.semaphore_signal(barrier, inc=1, device_id=sender, device_id_type=MESH)
+
+        @pl.when(tx == landing_tx[side])
+        def _():
+            relay = {"mode": mirror, "ty": ty, "tx": relay_tx[side]}
+            pl.semaphore_signal(barrier, inc=1, device_id=relay, device_id_type=MESH)
+
+    for step in range(1, modes):
+        pl.semaphore_signal(barrier, inc=1, device_id=peer(step), device_id_type=MESH)
+    object_loads = [pltpu.make_async_copy(obj_in.at[s], obj.at[s], load.at[3 + s]) for s in range(SLICES)]
     loads = [pltpu.make_async_copy(src, dst, load.at[i]) for i, (src, dst) in enumerate(((probe_in, probe), (mats_in, mats), (measured_in, measured)))]
-    for copy in loads:
+    for copy in object_loads + loads:
         copy.start()
 
     for side in (LEFT, RIGHT):
@@ -172,46 +208,15 @@
             gv[side - UP] = jnp.zeros_like(gv[side - UP])
             gc[side - UP] = jnp.zeros_like(gc[side - UP])
 
-    for s in range(SLICES):
+    def pack(s):
+        object_loads[s].wait()
         for c in range(2):
             for b in range(2):
                 left_edge, right_edge = packed_edges(obj[s, c, b * HALF : (b + 1) * HALF])
                 pk[s, LEFT, c, b * BLOCK : (b + 1) * BLOCK] = left_edge
                 pk[s, RIGHT, c, b * BLOCK : (b + 1) * BLOCK] = right_edge
 
-    barrier = pltpu.get_barrier_semaphore()
-    count = jnp.int32(modes - 1)
-    for side in (LEFT, RIGHT, UP, DOWN):
-        count = count + has[side].astype(jnp.int32)
-
-        @pl.when(has[side])
-        def _():
-            pl.semaphore_signal(barrier, inc=1, device_id=target[side], device_id_type=MESH)
-
-    for side, cross in ((LEFT, cross_left), (RIGHT, cross_right)):
-        far_pair = jnp.logical_and(cross, has[side])
-        count = count + far_pair.astype(jnp.int32)
-
-        @pl.when(far_pair)
-        def _():
-            pl.semaphore_signal(barrier, inc=1, device_id=direct[side], device_id_type=MESH)
-
-    for side in (LEFT, RIGHT):
-        from_relay, from_landing = crossing[side], relaying[side]
-        count = count + from_relay.astype(jnp.int32) + from_landing.astype(jnp.int32)
-
-        @pl.when(relaying[side])
-        def _():
-            sender = {"mode": mode, "ty": ty, "tx": landing_tx[1 - side]}
-            pl.semaphore_signal(barrier, inc=1, device_id=sender, device_id_type=MESH)
-
-        @pl.when(tx == landing_tx[side])
-        def _():
-            relay = {"mode": mirror, "ty": ty, "tx": relay_tx[side]}
-            pl.semaphore_signal(barrier, inc=1, device_id=relay, device_id_type=MESH)
-
-    for step in range(1, modes):
-        pl.semaphore_signal(barrier, inc=1, device_id=peer(step), device_id_type=MESH)
+    pack(0)
     pl.semaphore_wait(barrier, count)
 
     opposite = {LEFT: RIGHT, RIGHT: LEFT, UP: DOWN, DOWN: UP, UP_CORNER: DOWN_CORNER, DOWN_CORNER: UP_CORNER}
@@ -240,19 +245,19 @@
             device_id_type=MESH,
         )
 
-    def straight_copy(s, kind):
-        return pltpu.make_async_remote_copy(
-            src_ref=pk.at[s, kind, 0],
-            dst_ref=rs.at[s, opposite[kind], 0],
-            send_sem=cross_send.at[s, 0],
-            recv_sem=cross_recv.at[s, 0],
+    def straight_copy(s, kind, i):
+        return pltpu.make_async_remote_copy(
+            src_ref=pk.at[(s, kind, *STRAIGHT[i])],
+            dst_ref=rs.at[(s, opposite[kind], *STRAIGHT[i])],
+            send_sem=cross_send.at[s, 2 * i],
+            recv_sem=cross_recv.at[s, 2 * i],
             device_id=target[kind],
             device_id_type=MESH,
         )
 
     def detour_copy(s, kind):
         return pltpu.make_async_remote_copy(
-            src_ref=pk.at[s, kind, 1],
+            src_ref=pk.at[s, kind, 1, EXTRA:],
             dst_ref=rl.at[s],
             send_sem=cross_send.at[s, 1],
             recv_sem=relay_recv.at[s],
@@ -263,7 +268,7 @@
     def onward_copy(s, kind):
         return pltpu.make_async_remote_copy(
             src_ref=rl.at[s],
-            dst_ref=rs.at[s, opposite[kind], 1],
+            dst_ref=rs.at[s, opposite[kind], 1, EXTRA:],
             send_sem=relay_send.at[s],
             recv_sem=cross_recv.at[s, 1],
             device_id={"mode": mirror, "ty": ty, "tx": landing_tx[kind]},
@@ -282,7 +287,8 @@
 
             @pl.when(crossing[kind])
             def _():
-                straight_copy(s, kind).start()
+                straight_copy(s, kind, 0).start()
+                straight_copy(s, kind, 1).start()
                 detour_copy(s, kind).start()
 
     def await_halo(s, kind):
@@ -294,7 +300,8 @@
 
             @pl.when(crossing[kind])
             def _():
-                straight_copy(s, opposite[kind]).wait_recv()
+                straight_copy(s, opposite[kind], 0).wait_recv()
+                straight_copy(s, opposite[kind], 1).wait_recv()
                 onward_copy(s, opposite[kind]).wait_recv()
 
     def relay(s):
@@ -306,7 +313,9 @@
                 onward_copy(s, kind).start()
 
     for s in range(SLICES):
-        for kind in (LEFT, RIGHT, UP, DOWN):
+        if s + 1 < SLICES:
+            pack(s + 1)
+        for kind in (RIGHT, LEFT, UP, DOWN):
             start_halo(s, kind)
 
     def relay_corners(s):
@@ -356,13 +365,13 @@
             band = dot(twice(pick_rows, 1), both(ext[c], 0))
             window[s, c] = dot(both(band, 1), twice(put_cols, 0))
 
+    relay(0)
     relay_corners(0)
-    relay(0)
     for s in range(SLICES):
         if s + 1 < SLICES:
             relay_corners(s + 1)
-        for ahead in range(2 * s, min(2 * s + 2, SLICES)):
-            if ahead:
+        if s == 0:
+            for ahead in range(1, SLICES):
                 relay(ahead)
         build_window(s)
         if s == 0:
@@ -448,10 +457,10 @@
             device_id_type=MESH,
         )
 
-    def send_far(low_pair, i):
+    def send_far(low_pair, i, pieces=(0, 1, 2, 3)):
         @pl.when(first if low_pair else last)
         def _():
-            for q in range(4):
+            for q in pieces:
                 collect_copy(low_pair, i, q).start()
 
     def send_partner(owner):
@@ -459,9 +468,9 @@
         def _():
             partner_copy(owner).start()
 
-    def join(low_pair, i):
+    def join(low_pair, i, pieces=(0, 1, 2, 3)):
         s = far_slice(low_pair, i)
-        for q in range(4):
+        for q in pieces:
             collect_copy(low_pair, i, q).wait_recv()
             at = piece(q)
             joint[(i, *at)] = collected[(i, *at)] + term[(s, *at)]
@@ -496,18 +505,24 @@
             send_far(True, 1)
         elif s == 1:
             send_partner(1)
+            send_far(False, 0, (0, 1))
         else:
             send_far(False, 1)
             send_partner(0)
-            send_far(False, 0)
+            send_far(False, 0, (2, 3))
             send_partner(2)
 
     for low_pair in (True, False):
 
         @pl.when(mode == (1 if low_pair else 2))
         def _():
-            join(low_pair, 0 if low_pair else 1)
-            join(low_pair, 1 if low_pair else 0)
+            join(low_pair, 0, (0, 1))
+            if low_pair:
+                join(low_pair, 0, (2, 3))
+                join(low_pair, 1)
+            else:
+                join(low_pair, 1)
+                join(low_pair, 0, (2, 3))
 
     partner_copy(0).wait_recv()
     for q in range(4):
@@ -545,7 +560,7 @@
             device_id_type=MESH,
         )
 
-    directions = [(None, 0), (None, 1), (0, 0), (0, 1), (1, 0), (1, 1), (0, None), (1, None)]
+    directions = [(None, 1), (0, 1), (1, 1), (None, 0), (0, 0), (1, 0), (0, None), (1, None)]
     for v, h in directions:
 
         @pl.when(grad_has(v, h))
@@ -582,7 +597,8 @@
         @pl.when(crossing[kind])
         def _():
             for s in range(SLICES):
-                straight_copy(s, kind).wait_send()
+                straight_copy(s, kind, 0).wait_send()
+                straight_copy(s, kind, 1).wait_send()
                 detour_copy(s, kind).wait_send()
 
         @pl.when(relaying[kind])
@@ -617,12 +633,13 @@
     dma = pltpu.SemaphoreType.DMA
     wave = (LOCAL * DET, DET)
     scratch = dict(
+        obj=(SLICES, 2, DET, DET),
         probe=(LOCAL, 2, DET, DET),
         measured=(1, 1, 1, DET, DET),
         mats=(8, 2 * DET, 2 * DET),
         pk=(SLICES, 2, 2, HALF, DET),
         rs=(SLICES, 2, 2, HALF, DET),
-        rl=(SLICES, HALF, DET),
+        rl=(SLICES, HALF - EXTRA, DET),
         vt=(SLICES, 2, 2, HALF, DET),
         cr=(SLICES, 2, 2, 2, BLOCK, DET),
         ext=(2, 2 * DET, 2 * DET),
@@ -648,12 +665,12 @@
     return pl.pallas_call(
         kernel,
         out_shape=jax.ShapeDtypeStruct((1, 2, DET, DET), F32),
-        in_specs=[SMEM, VMEM, ANY, ANY, ANY],
+        in_specs=[SMEM, ANY, ANY, ANY, ANY],
         out_specs=VMEM,
         scratch_shapes=[pltpu.VMEM(shape, BF16 if name in ("mid", "mats") else F32) for name, shape in scratch.items()]
-        + [dma((3,))]
+        + [dma((3 + SLICES,))]
         + [dma((SLICES, 6)), dma((SLICES, 6))]
-        + [dma((SLICES, 2)), dma((SLICES, 2)), dma((SLICES,)), dma((SLICES,))]
+        + [dma((SLICES, 3)), dma((SLICES, 3)), dma((SLICES,)), dma((SLICES,))]
         + [dma((modes - 1,)), dma((modes - 1,))]
         + [dma((2, 4)), dma((2, 4)), dma((2, 4)), dma((4,)), dma, dma]
         + [dma((8,)), dma((8,))],

time: 60 us -> 58.2 us (0.970)
  the two profiles are of different devices: /device:TPU:39 before, /device:TPU:7 now
where the time goes in v5:
time: 58.2 us; the launch traced here: 57.1 us
  Pallas kernels  55.5 us (95%)
  local copies, waits for them, and re-layouts  1.57 us (3%)
    pallas_call x1, Pallas kernels, body(): pl.pallas_call(kernel, out_shape=jax.ShapeDtypeStruct((1, 2, DET, DET), F...  55.5 us
    unnamed x1, local copies, waits for them, and re-layouts  1.57 us

profile of v5, /device:TPU:7, one launch (start us, length us, event | category | flops | bytes accessed | tf_op | source)
XLA Modules:
  0.0 57.1 jit_solution(438852568994625124)
XLA Ops:
  0.0 55.5 %ptycho.1 = f32[1,2,128,128]{3,2,1,0:T(8,128)} custom-call(s32[2]{0:T(128)} %bitcast.1, f32[4,2,128,128]{3,2,1,0:T(8,128)} %obj_in.1, f32[4,2,128,128]{3,2,1,0:T(8,128)} %probe_in.1, f32[1,1,1,128,128]{4,3,2,1,0:T(8,128)} %measured_in.1, bf16[8,256,256]{2,1,0:T(8,128)(2,1)} %constant.2.clone.mats_in), custom_call_target="tpu_custom_call" | custom-call | tf_op jit(solution)/shard_map/ptycho/pallas_call | solution.py:665
  55.5 1.6 %copy.7 = f32[1,2,128,128]{3,2,1,0:T(8,128)} copy(f32[1,2,128,128]{3,2,1,0:T(8,128)} %ptycho.1) | data formatting | bytes 262144

commit v6 on v5

--- a/solution.py
+++ b/solution.py
@@ -83,7 +83,7 @@
 MESH = pl.DeviceIdType.MESH
 HALF = DET // 2
 BLOCK = HALF // 2
-EXTRA = 8
+EXTRA = 16
 STRAIGHT = ((0, slice(0, HALF)), (1, slice(0, EXTRA)))
 
 
@@ -447,12 +447,12 @@
             device_id_type=MESH,
         )
 
-    def partner_copy(owner):
-        return pltpu.make_async_remote_copy(
-            src_ref=term.at[owner],
-            dst_ref=parts.at[0],
-            send_sem=partner_send,
-            recv_sem=partner_recv,
+    def partner_copy(owner, c):
+        return pltpu.make_async_remote_copy(
+            src_ref=term.at[owner, c],
+            dst_ref=parts.at[0, c],
+            send_sem=partner_send.at[c],
+            recv_sem=partner_recv.at[c],
             device_id={"mode": owner, "ty": ty, "tx": tx},
             device_id_type=MESH,
         )
@@ -466,7 +466,8 @@
     def send_partner(owner):
         @pl.when(mode == (owner ^ 1))
         def _():
-            partner_copy(owner).start()
+            for c in range(2):
+                partner_copy(owner, c).start()
 
     def join(low_pair, i, pieces=(0, 1, 2, 3)):
         s = far_slice(low_pair, i)
@@ -524,12 +525,11 @@
                 join(low_pair, 1)
                 join(low_pair, 0, (2, 3))
 
-    partner_copy(0).wait_recv()
-    for q in range(4):
-        pair_sum_copy(True, 0, q).wait_recv()
-    for c in range(2):
-        mine = term[mode, c]
-        mine = mine + parts[0, c] + parts[1, c]
+    def place(c):
+        partner_copy(0, c).wait_recv()
+        for q in range(2 * c, 2 * c + 2):
+            pair_sum_copy(True, 0, q).wait_recv()
+        mine = term[mode, c] + parts[0, c] + parts[1, c]
         tall = dot(twice(put_rows, 1), both(mine, 0))
         placed = dot(both(tall, 1), twice(pick_cols, 0))
         middle[c] = placed[HALF : 3 * HALF, :DET]
@@ -544,33 +544,36 @@
             return has[h]
         return has[UP + v] if h is None else jnp.logical_and(has[UP + v], has[h])
 
-    def grad_copy(v, h):
+    def grad_copy(v, h, c):
         if v is None:
-            src, dst, i = hp.at[h], gh.at[1 - h], h
+            src, dst, i = hp.at[h, c], gh.at[1 - h, c], h
         elif h is None:
-            src, dst, i = vp.at[v], gv.at[1 - v], 2 + v
+            src, dst, i = vp.at[v, c], gv.at[1 - v, c], 2 + v
         else:
-            src, dst, i = cp.at[v, h], gc.at[1 - v, 1 - h], 4 + 2 * v + h
+            src, dst, i = cp.at[v, h, c], gc.at[1 - v, 1 - h, c], 4 + 2 * v + h
         return pltpu.make_async_remote_copy(
             src_ref=src,
             dst_ref=dst,
-            send_sem=grad_send.at[i],
-            recv_sem=grad_recv.at[i],
+            send_sem=grad_send.at[i, c],
+            recv_sem=grad_recv.at[i, c],
             device_id={"mode": mode, "ty": ty if v is None else ty + 2 * v - 1, "tx": tx if h is None else tx + 2 * h - 1},
             device_id_type=MESH,
         )
 
     directions = [(None, 1), (0, 1), (1, 1), (None, 0), (0, 0), (1, 0), (0, None), (1, None)]
-    for v, h in directions:
-
-        @pl.when(grad_has(v, h))
-        def _():
-            grad_copy(v, h).start()
+    for c in range(2):
+        place(c)
+        for v, h in directions:
+
+            @pl.when(grad_has(v, h))
+            def _():
+                grad_copy(v, h, c).start()
 
     for v, h in reversed(directions):
         @pl.when(grad_has(v, h))
         def _():
-            grad_copy(v if v is None else 1 - v, h if h is None else 1 - h).wait_recv()
+            for c in range(2):
+                grad_copy(v if v is None else 1 - v, h if h is None else 1 - h, c).wait_recv()
 
     for c in range(2):
         for v in range(2):
@@ -583,7 +586,8 @@
 
         @pl.when(grad_has(v, h))
         def _():
-            grad_copy(v, h).wait_send()
+            for c in range(2):
+                grad_copy(v, h, c).wait_send()
 
     for kind in range(6):
 
@@ -609,7 +613,8 @@
     for step in range(1, modes):
         mode_copy(step).wait_send()
 
-    partner_copy(0).wait_send()
+    for c in range(2):
+        partner_copy(0, c).wait_send()
     for i in range(2):
         for q in range(4):
 
@@ -672,8 +677,8 @@
         + [dma((SLICES, 6)), dma((SLICES, 6))]
         + [dma((SLICES, 3)), dma((SLICES, 3)), dma((SLICES,)), dma((SLICES,))]
         + [dma((modes - 1,)), dma((modes - 1,))]
-        + [dma((2, 4)), dma((2, 4)), dma((2, 4)), dma((4,)), dma, dma]
-        + [dma((8,)), dma((8,))],
+        + [dma((2, 4)), dma((2, 4)), dma((2, 4)), dma((4,)), dma((2,)), dma((2,))]
+        + [dma((8, 2)), dma((8, 2))],
         compiler_params=pltpu.CompilerParams(collective_id=0, has_side_effects=True),
         name="ptycho",
     )(positions.reshape(2), object_slices, probe_modes, measured, mats)

time: 58.2 us -> 57.4 us (0.986)
  Pallas kernels: 55.5 us -> 54.8 us
    pallas_call x1, Pallas kernels: 55.5 us -> 54.8 us  [body(): pl.pallas_call(kernel, out_shape=jax.ShapeDtypeStruct((1, 2, DET, DET), F...]
where the time goes in v6:
time: 57.4 us; the launch traced here: 56.3 us
  Pallas kernels  54.8 us (95%)
  local copies, waits for them, and re-layouts  1.57 us (3%)
    pallas_call x1, Pallas kernels, body(): pl.pallas_call(kernel, out_shape=jax.ShapeDtypeStruct((1, 2, DET, DET), F...  54.8 us
    unnamed x1, local copies, waits for them, and re-layouts  1.57 us

profile of v6, /device:TPU:7, one launch (start us, length us, event | category | flops | bytes accessed | tf_op | source)
XLA Modules:
  0.0 56.3 jit_solution(3167178450286469016)
XLA Ops:
  0.0 54.8 %ptycho.1 = f32[1,2,128,128]{3,2,1,0:T(8,128)} custom-call(s32[2]{0:T(128)} %bitcast.1, f32[4,2,128,128]{3,2,1,0:T(8,128)} %obj_in.1, f32[4,2,128,128]{3,2,1,0:T(8,128)} %probe_in.1, f32[1,1,1,128,128]{4,3,2,1,0:T(8,128)} %measured_in.1, bf16[8,256,256]{2,1,0:T(8,128)(2,1)} %constant.2.clone.mats_in), custom_call_target="tpu_custom_call" | custom-call | tf_op jit(solution)/shard_map/ptycho/pallas_call | solution.py:670
  54.8 1.6 %copy.7 = f32[1,2,128,128]{3,2,1,0:T(8,128)} copy(f32[1,2,128,128]{3,2,1,0:T(8,128)} %ptycho.1) | data formatting | bytes 262144

commit v7 on v6

--- a/solution.py
+++ b/solution.py
@@ -411,8 +411,8 @@
             device_id_type=MESH,
         )
 
-    for step in range(1, modes):
-        mode_copy(step).start()
+    for peer_mode in (jnp.where(lower, 3, 0), jnp.where(lower, 2, 1), mode + 1 - 2 * lax.rem(mode, 2)):
+        mode_copy(lax.rem(peer_mode - mode + modes, modes)).start()
     whole = part[...]
     for step in range(1, modes):
         mode_copy(step).wait_recv()

time: 57.4 us -> 56.1 us (0.977)
  Pallas kernels: 54.8 us -> 53.8 us
    pallas_call x1, Pallas kernels: 54.8 us -> 53.8 us  [body(): pl.pallas_call(kernel, out_shape=jax.ShapeDtypeStruct((1, 2, DET, DET), F...]
where the time goes in v7:
time: 56.1 us; the launch traced here: 55.3 us
  Pallas kernels  53.8 us (96%)
  local copies, waits for them, and re-layouts  1.57 us (3%)
    pallas_call x1, Pallas kernels, body(): pl.pallas_call(kernel, out_shape=jax.ShapeDtypeStruct((1, 2, DET, DET), F...  53.8 us
    unnamed x1, local copies, waits for them, and re-layouts  1.57 us

profile of v7, /device:TPU:7, one launch (start us, length us, event | category | flops | bytes accessed | tf_op | source)
XLA Modules:
  0.0 55.3 jit_solution(14383081125537234091)
XLA Ops:
  0.0 53.8 %ptycho.1 = f32[1,2,128,128]{3,2,1,0:T(8,128)} custom-call(s32[2]{0:T(128)} %bitcast.1, f32[4,2,128,128]{3,2,1,0:T(8,128)} %obj_in.1, f32[4,2,128,128]{3,2,1,0:T(8,128)} %probe_in.1, f32[1,1,1,128,128]{4,3,2,1,0:T(8,128)} %measured_in.1, bf16[8,256,256]{2,1,0:T(8,128)(2,1)} %constant.2.clone.mats_in), custom_call_target="tpu_custom_call" | custom-call | tf_op jit(solution)/shard_map/ptycho/pallas_call | solution.py:670
  53.8 1.6 %copy.7 = f32[1,2,128,128]{3,2,1,0:T(8,128)} copy(f32[1,2,128,128]{3,2,1,0:T(8,128)} %ptycho.1) | data formatting | bytes 262144

commit v8 on v7

--- a/solution.py
+++ b/solution.py
@@ -68,17 +68,22 @@
 
 
 def two_sided(mats, which, fetch, deliver, mid):
-    for m in range(LOCAL):
-        real, imag = fetch(m)
+    kept = []
+    for pair in range(LOCAL // 2):
+        got = [fetch(m) for m in (2 * pair, 2 * pair + 1)]
+        real = jnp.concatenate([g[0] for g in got], axis=0)
+        imag = jnp.concatenate([g[1] for g in got], axis=0)
         out = right_product(mats, which, real, imag)
-        rh, rl = halves(out[:, :DET])
-        ih, il = halves(out[:, DET:])
-        for part, value in enumerate((rh, ih, rl, il)):
-            mid[rows(part), rows(m)] = value
+        re = jnp.concatenate([out[:DET, :DET], out[DET:, :DET]], axis=1)
+        im = jnp.concatenate([out[:DET, DET:], out[DET:, DET:]], axis=1)
+        stack = jnp.concatenate([re, im], axis=0)
+        high, low = halves(stack)
+        kept.append(jnp.concatenate([high, low], axis=0))
     for pair in range(LOCAL // 2):
-        out = left_product(mats, which, mid[:, pair * 2 * DET : (pair + 1) * 2 * DET])
+        out = left_product(mats, which, kept[pair])
         for k in range(2):
             deliver(2 * pair + k, out[:DET, rows(k)], out[DET:, rows(k)])
+
 
 MESH = pl.DeviceIdType.MESH
 HALF = DET // 2
@@ -679,7 +684,7 @@
         + [dma((modes - 1,)), dma((modes - 1,))]
         + [dma((2, 4)), dma((2, 4)), dma((2, 4)), dma((4,)), dma((2,)), dma((2,))]
         + [dma((8, 2)), dma((8, 2))],
-        compiler_params=pltpu.CompilerParams(collective_id=0, has_side_effects=True),
+        compiler_params=pltpu.CompilerParams(collective_id=0, has_side_effects=True, vmem_limit_bytes=55000 * 1024),
         name="ptycho",
     )(positions.reshape(2), object_slices, probe_modes, measured, mats)
 

time: 56.1 us -> 56 us (level)
  Pallas kernels: 53.8 us -> 53 us
  local copies, waits for them, and re-layouts: 1.57 us -> 2.15 us
    pallas_call x1, Pallas kernels: 53.8 us -> 53 us  [body(): pl.pallas_call(kernel, out_shape=jax.ShapeDtypeStruct((1, 2, DET, DET), F...]
    unnamed x1 -> x5, local copies, waits for them, and re-layouts: 1.57 us -> 2.15 us
where the time goes in v8:
time: 56 us; the launch traced here: 55.2 us
  Pallas kernels  53 us (95%)
  local copies, waits for them, and re-layouts  2.15 us (4%)
    pallas_call x1, Pallas kernels, body(): pl.pallas_call(kernel, out_shape=jax.ShapeDtypeStruct((1, 2, DET, DET), F...  53 us
    unnamed x5, local copies, waits for them, and re-layouts  2.15 us

profile of v8, /device:TPU:7, one launch (start us, length us, event | category | flops | bytes accessed | tf_op | source)
XLA Modules:
  0.0 55.2 jit_solution(2395151168378107611)
XLA Ops:
  0.0 0.0 copy-start.1
  0.0 0.7 %copy-done.1 = s32[1,1,1,2]{3,2,1,0:T(1,128)S(1)} copy-done((s32[1,1,1,2]{3,2,1,0:T(1,128)S(1)}, s32[1,1,1,2]{3,2,1,0:T(1,128)}, u32[]{:S(2)}) %copy-start.1) | copy-done | bytes 32
  0.7 0.0 copy-start
  0.7 0.8 %copy-done = f32[1,1,1,128,128]{4,3,2,1,0:T(8,128)S(1)} copy-done((f32[1,1,1,128,128]{4,3,2,1,0:T(8,128)S(1)}, f32[1,1,1,128,128]{4,3,2,1,0:T(8,128)}, u32[]{:S(2)}) %copy-start) | copy-done | bytes 65560
  1.5 53.0 %ptycho.1 = f32[1,2,128,128]{3,2,1,0:T(8,128)S(1)} custom-call(s32[2]{0:T(128)S(1)} %bitcast.1, f32[4,2,128,128]{3,2,1,0:T(8,128)} %obj_in.1, f32[4,2,128,128]{3,2,1,0:T(8,128)} %probe_in.1, f32[1,1,1,128,128]{4,3,2,1,0:T(8,128)S(1)} %copy-done, bf16[8,256,256]{2,1,0:T(8,128)(2,1)} %constant.2.clone.mats_in), custom_call_target="tpu_custom_call" | custom-call | tf_op jit(solution)/shard_map/ptycho/pallas_call | solution.py:675
  54.5 0.7 %copy.7 = f32[1,2,128,128]{3,2,1,0:T(8,128)} copy(f32[1,2,128,128]{3,2,1,0:T(8,128)S(1)} %ptycho.1) | data formatting | bytes 262144
Async XLA Ops:
  0.0 0.7 %copy-start.1 = (s32[1,1,1,2]{3,2,1,0:T(1,128)S(1)}, s32[1,1,1,2]{3,2,1,0:T(1,128)}, u32[]{:S(2)}) copy-start(s32[1,1,1,2]{3,2,1,0:T(1,128)} %param.7) | copy-start | bytes 28
  0.7 0.8 %copy-start = (f32[1,1,1,128,128]{4,3,2,1,0:T(8,128)S(1)}, f32[1,1,1,128,128]{4,3,2,1,0:T(8,128)}, u32[]{:S(2)}) copy-start(f32[1,1,1,128,128]{4,3,2,1,0:T(8,128)} %measured_in.1) | copy-start | bytes 196612

commit v9 on v7

--- a/solution.py
+++ b/solution.py
@@ -563,11 +563,17 @@
     directions = [(None, 1), (0, 1), (1, 1), (None, 0), (0, 0), (1, 0), (0, None), (1, None)]
     for c in range(2):
         place(c)
-        for v, h in directions:
-
-            @pl.when(grad_has(v, h))
-            def _():
-                grad_copy(v, h, c).start()
+        for early in (True, False):
+            for v, h in directions:
+                if h is None and early:
+                    continue
+                when = grad_has(v, h)
+                if h is not None:
+                    when = jnp.logical_and(when, crossing[h] if early else jnp.logical_not(crossing[h]))
+
+                @pl.when(when)
+                def _():
+                    grad_copy(v, h, c).start()
 
     for v, h in reversed(directions):
         @pl.when(grad_has(v, h))

time: 56.1 us -> 56.2 us (level)
  no operation moved by 1% of the time
where the time goes in v9:
time: 56.2 us; the launch traced here: 55.4 us
  Pallas kernels  53.8 us (96%)
  local copies, waits for them, and re-layouts  1.57 us (3%)
    pallas_call x1, Pallas kernels, body(): pl.pallas_call(kernel, out_shape=jax.ShapeDtypeStruct((1, 2, DET, DET), F...  53.8 us
    unnamed x1, local copies, waits for them, and re-layouts  1.57 us

profile of v9, /device:TPU:7, one launch (start us, length us, event | category | flops | bytes accessed | tf_op | source)
XLA Modules:
  0.0 55.4 jit_solution(3921889058297129183)
XLA Ops:
  0.0 53.8 %ptycho.1 = f32[1,2,128,128]{3,2,1,0:T(8,128)} custom-call(s32[2]{0:T(128)} %bitcast.1, f32[4,2,128,128]{3,2,1,0:T(8,128)} %obj_in.1, f32[4,2,128,128]{3,2,1,0:T(8,128)} %probe_in.1, f32[1,1,1,128,128]{4,3,2,1,0:T(8,128)} %measured_in.1, bf16[8,256,256]{2,1,0:T(8,128)(2,1)} %constant.2.clone.mats_in), custom_call_target="tpu_custom_call" | custom-call | tf_op jit(solution)/shard_map/ptycho/pallas_call | solution.py:676
  53.8 1.6 %copy.7 = f32[1,2,128,128]{3,2,1,0:T(8,128)} copy(f32[1,2,128,128]{3,2,1,0:T(8,128)} %ptycho.1) | data formatting | bytes 262144
